TPU v7x, 256 devices: a whole 4x4x8 slice. The times are simulated.
256 devices in a mesh: tile: 4 (over x), expert: 64 (over y, z, core).
Axes of the slice: x: 4, y: 4, z: 8, core: 2. Of those that a mesh axis runs over, the one named last changes fastest.
Arguments:
- patches: bfloat16 [64, 16, 32, 1152], P('expert', 'tile'), may hold values from -6 to 6
- norm1_gain: float32 [1152], replicated, may hold values from 0.1 to 1.9
- qkv_weight: bfloat16 [1152, 3, 1152], P(None, None, 'tile'), may hold values from -8 to 8
- qkv_bias: float32 [3, 1152], P(None, 'tile'), may hold values from -3 to 3
- out_weight: bfloat16 [1152, 1152], P('tile'), may hold values from -0.1875 to 0.1875
- out_bias: float32 [1152], replicated, may hold values from -3 to 3
- norm2_gain: float32 [1152], replicated, may hold values from 0.1 to 1.9
- proj_weight: bfloat16 [4608, 2048], P('expert', 'tile'), may hold values from -0.09375 to 0.09375
- moe_gain: float32 [2048], replicated, may hold values from 0.1 to 1.9
- expert_in: bfloat16 [64, 2048, 2, 1408], P('expert', None, None, 'tile'), may hold values from -0.125 to 0.125
- expert_out: bfloat16 [64, 1408, 2048], P('expert', 'tile'), may hold values from -0.15625 to 0.15625
- shared_in: bfloat16 [2048, 2, 1408], P(None, None, 'tile'), may hold values from -0.125 to 0.125
- shared_out: bfloat16 [1408, 2048], P('tile'), may hold values from -0.15625 to 0.15625
- routes: int32 [64, 8, 16, 6], P('expert'), may hold values from 0 to 63, all different within a row; in each aligned block of 32 rows (0 to 31, 32 to 63, ..., all dimensions but the last counted through in order) at most 6 rows name the same one
- gates: float32 [64, 8, 16, 6], P('expert', 'tile'), may hold values from 0.1 to 1
Outputs:
- moe_tokens: bfloat16 [64, 8, 16, 2048], P('expert', 'tile')
Inputs may be any that keep to these rules, and one draw needn't show every extreme that they name: `routes`: each merged token names 6 different experts. Flattening the merged tokens in the order page, row, column into aligned blocks of 32 (the merged tokens of one device), no expert is named more than 6 times in a block, a bound that some block reaches.
All inputs are finite; a program needn't handle non-finite values.
Results may differ from a plain program's by a relative error of at most 0.02.
Values may be sent and summed in bfloat16 or wider, within the bound.
A program may use at most 128 MiB of HBM per device.

v0:
```python
import math

import jax
import jax.numpy as jnp
from jax import lax
from jax.experimental import pallas as pl
from jax.experimental.pallas import tpu as pltpu
from jax.sharding import PartitionSpec as P


HD = 72
NX, NY, NZ, NC = 4, 4, 8, 2
GROUP = NY * NC
CAP = 6
MESH = pl.DeviceIdType.MESH

norm_eps = 1e-06
rope_base = 10000.0


def layer_norm(values, gain_vec):
    centre = values - jnp.mean(values, axis=-1, keepdims=True)
    spread = jnp.mean(centre * centre, axis=-1, keepdims=True)
    return centre * lax.rsqrt(spread + norm_eps) * gain_vec


def rms_norm(values, gain_vec):
    return (
        values * lax.rsqrt(jnp.mean(values * values, axis=-1, keepdims=True) + norm_eps) * gain_vec
    )


def rope_tables(positions, columns, head_size):
    quarter = head_size // 4
    inverse = jnp.exp(jnp.arange(quarter).astype(jnp.float32) * (-math.log(rope_base) / quarter))
    row_angle = (positions // columns).astype(jnp.float32)[:, None] * inverse[None, :]
    col_angle = (positions % columns).astype(jnp.float32)[:, None] * inverse[None, :]
    return (jnp.cos(row_angle), jnp.sin(row_angle), jnp.cos(col_angle), jnp.sin(col_angle))


def rotate(values, tables):
    cos_row, sin_row, cos_col, sin_col = tables
    quarter = values.shape[-1] // 4
    row_a = values[..., :quarter]
    row_b = values[..., quarter : 2 * quarter]
    col_a = values[..., 2 * quarter : 3 * quarter]
    col_b = values[..., 3 * quarter :]
    return jnp.concatenate(
        [
            row_a * cos_row[:, None] - row_b * sin_row[:, None],
            row_b * cos_row[:, None] + row_a * sin_row[:, None],
            col_a * cos_col[:, None] - col_b * sin_col[:, None],
            col_b * cos_col[:, None] + col_a * sin_col[:, None],
        ],
        axis=-1,
    )


def attend(query_rows, key_rows, value_rows, divisor):
    scores = (
        jnp.einsum("qhd,khd->hqk", query_rows, key_rows, preferred_element_type=jnp.float32)
        / divisor
    )
    weights = jax.nn.softmax(scores, axis=-1).astype(jnp.bfloat16)
    attended = jnp.einsum(
        "hqk,khd->qhd", weights, value_rows, preferred_element_type=jnp.float32
    ).astype(jnp.bfloat16)
    return attended.reshape(attended.shape[0], -1)


def ring_place(axis):
    if axis == "x":
        return lax.axis_index("tile"), NX, lambda place: {"tile": place}
    here = lax.axis_index("expert")
    y, z, core = here // (NZ * NC), (here // NC) % NZ, here % NC
    return z, NZ, lambda place: {"expert": (y * NZ + place) * NC + core}


def greet(device_ids):
    barrier = pltpu.get_barrier_semaphore()
    for device_id in device_ids:
        pl.semaphore_signal(barrier, inc=1, device_id=device_id, device_id_type=MESH)
    pl.semaphore_wait(barrier, len(device_ids))


def ring_chunks(rows, step):
    starts = list(range(0, rows, step))
    half = (len(starts) + 1) // 2
    return [(s, step, 1 if i < half else -1) for i, s in enumerate(starts)]


def dir_order(chunks, sign):
    ids = range(len(chunks))
    return [i for i in ids if chunks[i][2] == sign] + [i for i in ids if chunks[i][2] != sign]


def interleave(a, b):
    out = []
    for i in range(max(len(a), len(b))):
        out += a[i : i + 1] + b[i : i + 1]
    return out


def ring_gather_kernel(plan, *refs):
    count = len(plan)
    ins, outs = refs[:count], refs[count : 2 * count]
    send_sem, recv_sem, local_sem = refs[2 * count :]
    rings = {axis: ring_place(axis) for axis, _ in plan}
    greet(
        [
            device((here + sign) % size)
            for here, size, device in rings.values()
            for sign in (1, -1)
        ]
    )
    arrivals, sends, number = {}, [], 0
    longest = max(rings[axis][1] // 2 for axis, _ in plan)
    local = []
    for hop in range(1, longest + 1):
        for task, (axis, chunks) in enumerate(plan):
            here, size, device = rings[axis]
            if hop > size // 2:
                continue
            order = interleave(
                [(1, i) for i in dir_order(chunks, 1)], [(-1, i) for i in dir_order(chunks, -1)]
            )
            for sign, i in order:
                start, rows, far = chunks[i]
                if hop == size // 2 and far != sign:
                    continue
                block = (here - sign * (hop - 1) + size) % size
                part = pl.ds(start, rows)
                if hop == 1:
                    source = ins[task].at[part]
                else:
                    arrivals.pop((task, sign, i)).wait_recv()
                    source = outs[task].at[block, part]
                copy = pltpu.make_async_remote_copy(
                    src_ref=source,
                    dst_ref=outs[task].at[block, part],
                    send_sem=send_sem.at[number],
                    recv_sem=recv_sem.at[number],
                    device_id=device((here + sign + size) % size),
                    device_id_type=MESH,
                )
                copy.start()
                arrivals[(task, sign, i)] = copy
                sends.append(copy)
                number += 1
        if hop == 1:
            for task, (axis, _) in enumerate(plan):
                own = pltpu.make_async_copy(
                    ins[task], outs[task].at[rings[axis][0]], local_sem.at[task]
                )
                own.start()
                local.append(own)
    for copy in arrivals.values():
        copy.wait_recv()
    for copy in sends:
        copy.wait_send()
    for own in local:
        own.wait()


def copies_of(axis, chunks):
    half = (NX if axis == "x" else NZ) // 2
    return sum(half + half - 1 for _ in chunks)


def ring_gather(tasks, collective_id):
    plan = [(axis, ring_chunks(block.shape[0], step)) for axis, block, step in tasks]
    copies = sum(copies_of(*entry) for entry in plan)
    sizes = {"x": NX, "z": NZ}

    def kernel(*refs):
        ring_gather_kernel(plan, *refs)

    return pl.pallas_call(
        kernel,
        out_shape=[
            jax.ShapeDtypeStruct((sizes[axis],) + block.shape, block.dtype)
            for axis, block, _ in tasks
        ],
        in_specs=[pl.BlockSpec(memory_space=pltpu.VMEM)] * len(tasks),
        out_specs=[pl.BlockSpec(memory_space=pltpu.VMEM)] * len(tasks),
        scratch_shapes=[
            pltpu.SemaphoreType.DMA((copies,)),
            pltpu.SemaphoreType.DMA((copies,)),
            pltpu.SemaphoreType.DMA((len(tasks),)),
        ],
        compiler_params=pltpu.CompilerParams(collective_id=collective_id, has_side_effects=True),
    )(*[block for _, block, _ in tasks])


def ring_reduce_kernel(plan, *refs):
    count = len(plan)
    ins, outs = refs[:count], refs[count : 2 * count]
    landed, staged = refs[2 * count : 3 * count], refs[3 * count : 4 * count]
    send_sem, recv_sem = refs[4 * count :]
    rings = {axis: ring_place(axis) for axis, _ in plan}
    greet(
        [
            device((here + sign + size) % size)
            for here, size, device in rings.values()
            for sign in (1, -1)
        ]
    )
    last, sends, number = {}, [], 0
    slots = [0] * count
    for step in range(max(rings[axis][1] // 2 for axis, _ in plan)):
        for task, (axis, chunks) in enumerate(plan):
            here, size, device = rings[axis]
            half = size // 2
            order = interleave(
                [(1, i) for i in dir_order(chunks, 1)], [(-1, i) for i in dir_order(chunks, -1)]
            )
            for sign, i in order:
                start, rows, far = chunks[i]
                length = half if far == sign else half - 1
                if step >= length:
                    continue
                part = pl.ds(start, rows)
                target = (here + sign * (length - step) + size) % size
                slot = slots[task]
                slots[task] += 1
                if step == 0:
                    source = ins[task].at[target, part]
                else:
                    copy, before = last[(task, sign, i)]
                    copy.wait_recv()
                    staged[task][slot] = (
                        ins[task][target, part].astype(jnp.float32)
                        + landed[task][before].astype(jnp.float32)
                    ).astype(staged[task].dtype)
                    source = staged[task].at[slot]
                copy = pltpu.make_async_remote_copy(
                    src_ref=source,
                    dst_ref=landed[task].at[slot],
                    send_sem=send_sem.at[number],
                    recv_sem=recv_sem.at[number],
                    device_id=device((here + sign + size) % size),
                    device_id_type=MESH,
                )
                copy.start()
                last[(task, sign, i)] = (copy, slot)
                sends.append(copy)
                number += 1
    for task, (axis, chunks) in enumerate(plan):
        here = rings[axis][0]
        for i, (start, rows, _) in enumerate(chunks):
            part = pl.ds(start, rows)
            total = ins[task][here, part].astype(jnp.float32)
            for sign in (1, -1):
                if (task, sign, i) in last:
                    copy, slot = last[(task, sign, i)]
                    copy.wait_recv()
                    total = total + landed[task][slot].astype(jnp.float32)
            outs[task][part] = total.astype(outs[task].dtype)
    for copy in sends:
        copy.wait_send()


def ring_reduce(tasks, collective_id):
    plan = [(axis, ring_chunks(block.shape[1], step)) for axis, block, step, _ in tasks]
    copies = [copies_of(*entry) for entry in plan]

    def kernel(*refs):
        ring_reduce_kernel(plan, *refs)

    boxes = [
        pltpu.VMEM((number, step, block.shape[2]), block.dtype)
        for number, (_, block, step, _) in zip(copies, tasks)
    ]
    return pl.pallas_call(
        kernel,
        out_shape=[jax.ShapeDtypeStruct(block.shape[1:], kind) for _, block, _, kind in tasks],
        in_specs=[pl.BlockSpec(memory_space=pltpu.VMEM)] * len(tasks),
        out_specs=[pl.BlockSpec(memory_space=pltpu.VMEM)] * len(tasks),
        scratch_shapes=boxes
        + boxes
        + [pltpu.SemaphoreType.DMA((sum(copies),)), pltpu.SemaphoreType.DMA((sum(copies),))],
        compiler_params=pltpu.CompilerParams(collective_id=collective_id, has_side_effects=True),
    )(*[block for _, block, _, _ in tasks])


CHUNKS = 4


def places():
    tile, here = lax.axis_index("tile"), lax.axis_index("expert")
    y, z, core = here // (NZ * NC), (here // NC) % NZ, here % NC
    across = {"tile": tile + 1 - 2 * (tile % 2)}, {"tile": NX - 1 - tile}

    def group(member):
        return {"expert": ((member // NC) * NZ + z) * NC + member % NC}

    def ring(place):
        return {"expert": (y * NZ + place) * NC + core}

    return tile, z, y * NC + core, across, group, ring


class Sender:
    def __init__(self, send_sem, recv_sem):
        self.send_sem, self.recv_sem, self.made = send_sem, recv_sem, []

    def send(self, source, target, device):
        number = len(self.made)
        copy = pltpu.make_async_remote_copy(
            src_ref=source,
            dst_ref=target,
            send_sem=self.send_sem.at[number],
            recv_sem=self.recv_sem.at[number],
            device_id=device,
            device_id_type=MESH,
        )
        copy.start()
        self.made.append(copy)
        return copy


Z_HALF = NZ // 2
Z_STREAMS = [(sign, half, Z_HALF if (half == 0) == (sign == 1) else Z_HALF - 1)
             for sign in (1, -1) for half in (0, 1)]
Z_STREAMS.sort(key=lambda stream: -stream[2])
X_HALF = NX // 2
X_STREAMS = [(sign, half, X_HALF if (half == 0) == (sign == 1) else X_HALF - 1)
             for sign in (1, -1) for half in (0, 1)]
X_STREAMS.sort(key=lambda stream: -stream[2])
Z_COPIES = sum(length for _, _, length in Z_STREAMS)
X_COPIES = sum(length for _, _, length in X_STREAMS)


def dispatch_kernel(
    rows_ref, select_ref, shared_ref, out_ref, sum_ref, ring_ref, chosen_ref, land_ref, stage_ref,
    send_sem, recv_sem, local_sem,
):
    tile, z, me, across, group, ring = places()
    tokens, width = rows_ref.shape
    chunk, half_rows = width // CHUNKS, tokens // 2
    post = Sender(send_sem, recv_sem)
    peers = [(me + k) % GROUP for k in range(1, GROUP)]
    greet(
        [ring((z + 1) % NZ), ring((z + NZ - 1) % NZ)]
        + [group(peer) for peer in peers]
        + list(across)
    )
    cols = [pl.ds(j * chunk, chunk) for j in range(CHUNKS)]
    part = [pl.ds(h * half_rows, half_rows) for h in (0, 1)]
    arrivals = {}

    def hop(j, number):
        for sign, half, length in Z_STREAMS:
            if number > length:
                continue
            block = (z - sign * (number - 1) + NZ) % NZ
            if number == 1:
                source = rows_ref.at[part[half], cols[j]]
            else:
                arrivals[(j, sign, half)].wait_recv()
                source = ring_ref.at[j, block, part[half]]
            arrivals[(j, sign, half)] = post.send(
                source, ring_ref.at[j, block, part[half]], ring((z + sign + NZ) % NZ)
            )

    for j in range(CHUNKS):
        hop(j, 1)

    sums = {}

    def shared_step(step):
        for sign, half, length in X_STREAMS:
            if step >= length:
                continue
            target = (tile + sign * (length - step) + NX) % NX
            slot = len(sums)
            if step == 0:
                source = shared_ref.at[target, part[half]]
            else:
                copy, before = sums[(sign, half, step - 1)]
                copy.wait_recv()
                stage_ref[slot] = (
                    shared_ref[target, part[half]].astype(jnp.float32)
                    + land_ref[before].astype(jnp.float32)
                ).astype(stage_ref.dtype)
                source = stage_ref.at[slot]
            copy = post.send(source, land_ref.at[slot], {"tile": (tile + sign + NX) % NX})
            sums[(sign, half, step)] = (copy, slot)

    shared_step(0)
    for j in range(CHUNKS):
        ring_ref[j, z] = rows_ref[:, j * chunk : (j + 1) * chunk]

    swaps, own = {}, []

    def hand_on(j, member, source):
        for side in (0, 1):
            post_to = out_ref.at[2 * side, member, :, cols[j]]
            handed.append(post.send(source, post_to, across[side]))

    handed = []

    def choose(j):
        for sign, half, _ in Z_STREAMS:
            arrivals[(j, sign, half)].wait_recv()
        gathered = ring_ref[j].reshape(NZ * tokens, chunk)
        chosen_ref[j] = (
            jnp.dot(select_ref[...], gathered, preferred_element_type=jnp.float32)
            .astype(chosen_ref.dtype)
            .reshape(chosen_ref.shape[1:])
        )
        for k, peer in enumerate(peers):
            swaps[(j, k)] = post.send(
                chosen_ref.at[j, peer], out_ref.at[1, me, :, cols[j]], group(peer)
            )
        copy = pltpu.make_async_copy(
            chosen_ref.at[j, me], out_ref.at[1, me, :, cols[j]], local_sem.at[j]
        )
        copy.start()
        own.append(copy)
        hand_on(j, me, chosen_ref.at[j, me])

    for wave in range(CHUNKS + Z_HALF - 1):
        for number in range(Z_HALF, 1, -1):
            j = wave - (number - 2)
            if 0 <= j < CHUNKS:
                hop(j, number)
        j = wave - (Z_HALF - 1)
        if wave == 0:
            shared_step(1)
        if 0 <= j < CHUNKS:
            choose(j)
    for j in range(CHUNKS):
        for k in range(GROUP - 1):
            swaps[(j, k)].wait_recv()
            source = (me - 1 - k + GROUP) % GROUP
            hand_on(j, source, out_ref.at[1, source, :, cols[j]])
    for half in (0, 1):
        total = shared_ref[tile, part[half]].astype(jnp.float32)
        for sign, this, length in X_STREAMS:
            if this == half:
                copy, slot = sums[(sign, half, length - 1)]
                copy.wait_recv()
                total = total + land_ref[slot].astype(jnp.float32)
        sum_ref[part[half]] = total
    for copy in handed:
        copy.wait_recv()
    for copy in post.made:
        copy.wait_send()
    for copy in own:
        copy.wait()


def dispatch(rows, select, shared_rows, collective_id):
    tokens, width = rows.shape
    slots = NZ * CAP
    chunk = width // CHUNKS
    copies = CHUNKS * (Z_COPIES + (GROUP - 1) + 2 * GROUP) + X_COPIES
    return pl.pallas_call(
        dispatch_kernel,
        out_shape=[
            jax.ShapeDtypeStruct((3, GROUP, slots, width), rows.dtype),
            jax.ShapeDtypeStruct((tokens, width), jnp.float32),
        ],
        in_specs=[pl.BlockSpec(memory_space=pltpu.VMEM)] * 3,
        out_specs=[pl.BlockSpec(memory_space=pltpu.VMEM)] * 2,
        scratch_shapes=[
            pltpu.VMEM((CHUNKS, NZ, tokens, chunk), rows.dtype),
            pltpu.VMEM((CHUNKS, GROUP, slots, chunk), rows.dtype),
            pltpu.VMEM((X_COPIES, tokens // 2, width), rows.dtype),
            pltpu.VMEM((X_COPIES, tokens // 2, width), rows.dtype),
            pltpu.SemaphoreType.DMA((copies,)),
            pltpu.SemaphoreType.DMA((copies,)),
            pltpu.SemaphoreType.DMA((CHUNKS,)),
        ],
        compiler_params=pltpu.CompilerParams(collective_id=collective_id, has_side_effects=True),
    )(rows, select, shared_rows)


def give_back_kernel(
    first_ref, second_ref, gated_ref, out_ref, high_ref, low_ref, side_ref, stage_ref, back_ref, mix_ref,
    land_ref, step_ref, send_sem, recv_sem,
):
    _, z, me, across, group, ring = places()
    tokens, width = out_ref.shape
    chunk, half_rows = width // CHUNKS, tokens // 2
    post = Sender(send_sem, recv_sem)
    peers = [(me + k) % GROUP for k in range(1, GROUP)]
    greet(
        [ring((z + 1) % NZ), ring((z + NZ - 1) % NZ)]
        + [group(peer) for peer in peers]
        + list(across)
    )
    cols = [pl.ds(j * chunk, chunk) for j in range(CHUNKS)]
    part = [pl.ds(h * half_rows, half_rows) for h in (0, 1)]
    order = peers + [me]
    sides, swaps, steps = {}, {}, {}
    for j in range(CHUNKS):
        for k, member in enumerate(order):
            for side, source in ((0, first_ref.at[0]), (1, second_ref.at[1])):
                sides[(j, k, side)] = post.send(
                    source.at[member, :, cols[j]], side_ref.at[side, j, member], across[side]
                )

    gated = gated_ref[...].T
    high = gated.astype(high_ref.dtype)
    high_ref[...] = high
    low_ref[...] = (gated - high.astype(jnp.float32)).astype(low_ref.dtype)

    def add_up(j):
        for k, member in enumerate(order):
            for side in (0, 1):
                sides[(j, k, side)].wait_recv()
            total = (
                first_ref[1, member, :, j * chunk : (j + 1) * chunk].astype(jnp.float32)
                + second_ref[0, member, :, j * chunk : (j + 1) * chunk].astype(jnp.float32)
                + side_ref[0, j, member].astype(jnp.float32)
                + side_ref[1, j, member].astype(jnp.float32)
            ).astype(stage_ref.dtype)
            if k == GROUP - 1:
                back_ref[j, member] = total
            else:
                stage_ref[j, member] = total
                swaps[(j, k)] = post.send(
                    stage_ref.at[j, member], back_ref.at[j, me], group(member)
                )

    def step(j, number):
        for i, (sign, half, length) in enumerate(Z_STREAMS):
            if number >= length:
                continue
            target = (z + sign * (length - number) + NZ) % NZ
            slot = i * Z_HALF + number
            if number == 0:
                source = mix_ref.at[j, target, part[half]]
            else:
                steps[(j, i, number - 1)].wait_recv()
                step_ref[j, slot] = (
                    mix_ref[j, target, part[half]].astype(jnp.float32)
                    + land_ref[j, slot - 1].astype(jnp.float32)
                ).astype(step_ref.dtype)
                source = step_ref.at[j, slot]
            steps[(j, i, number)] = post.send(
                source, land_ref.at[j, slot], ring((z + sign + NZ) % NZ)
            )

    def combine(j):
        for k in range(GROUP - 1):
            swaps[(j, k)].wait_recv()
        back = back_ref[j].reshape(high_ref.shape[1], chunk)
        mix_ref[j] = (
            (
                jnp.dot(high_ref[...], back, preferred_element_type=jnp.float32)
                + jnp.dot(low_ref[...], back, preferred_element_type=jnp.float32)
            )
            .astype(mix_ref.dtype)
            .reshape(mix_ref.shape[1:])
        )
        step(j, 0)

    def finish(j):
        for half in (0, 1):
            total = mix_ref[j, z, part[half]].astype(jnp.float32)
            for i, (_, this, length) in enumerate(Z_STREAMS):
                if this == half:
                    steps[(j, i, length - 1)].wait_recv()
                    total = total + land_ref[j, i * Z_HALF + length - 1].astype(jnp.float32)
            out_ref[half * half_rows : (half + 1) * half_rows, j * chunk : (j + 1) * chunk] = total

    for wave in range(CHUNKS + Z_HALF + 1):
        if wave < CHUNKS:
            add_up(wave)
        if 0 <= wave - 1 < CHUNKS:
            combine(wave - 1)
        for number in range(1, Z_HALF):
            if 0 <= wave - 1 - number < CHUNKS:
                step(wave - 1 - number, number)
    for j in range(CHUNKS):
        finish(j)
    for copy in post.made:
        copy.wait_send()


def give_back(first, second, gated, tokens, collective_id):
    width = first.shape[-1]
    slots = NZ * CAP
    chunk = width // CHUNKS
    copies = CHUNKS * (2 * GROUP + (GROUP - 1) + Z_COPIES)
    boxes = pltpu.VMEM((CHUNKS, len(Z_STREAMS) * Z_HALF, tokens // 2, chunk), first.dtype)
    blocks = pltpu.VMEM((CHUNKS, GROUP, slots, chunk), first.dtype)
    return pl.pallas_call(
        give_back_kernel,
        out_shape=jax.ShapeDtypeStruct((tokens, width), jnp.float32),
        in_specs=[pl.BlockSpec(memory_space=pltpu.VMEM)] * 3,
        out_specs=pl.BlockSpec(memory_space=pltpu.VMEM),
        scratch_shapes=[
            pltpu.VMEM(gated.shape[::-1], first.dtype),
            pltpu.VMEM(gated.shape[::-1], first.dtype),
            pltpu.VMEM((2, CHUNKS, GROUP, slots, chunk), first.dtype),
            blocks,
            blocks,
            pltpu.VMEM((CHUNKS, NZ, tokens, chunk), first.dtype),
            boxes,
            boxes,
            pltpu.SemaphoreType.DMA((copies,)),
            pltpu.SemaphoreType.DMA((copies,)),
        ],
        compiler_params=pltpu.CompilerParams(collective_id=collective_id, has_side_effects=True),
    )(first, second, gated)


def slot_tables(table, tokens, top):
    picks = table[:, :top, :tokens].transpose(1, 0, 2).reshape(top, NZ * tokens)
    gates = table[:, 8 : 8 + top, :tokens].transpose(1, 0, 2).reshape(top, NZ * tokens)
    z = (lax.axis_index("expert") // NC) % NZ
    member = jnp.arange(GROUP)
    experts = ((member // NC) * NZ + z) * NC + member % NC
    match = picks[None] == experts.astype(jnp.float32)[:, None, None]
    hit = jnp.any(match, axis=1)
    gate = jnp.sum(jnp.where(match, gates[None], 0.0), axis=1)
    column = jnp.arange(NZ * tokens)
    page = column // tokens
    earlier = (page[:, None] == page[None, :]) & (column[:, None] < column[None, :])
    rank = jnp.dot(
        hit.astype(jnp.bfloat16), earlier.astype(jnp.bfloat16), preferred_element_type=jnp.float32
    )
    slot = jnp.arange(NZ * CAP)
    here = (slot // CAP)[:, None] == page[None, :]
    ranked = rank[:, None, :] == (slot % CAP).astype(jnp.float32)[None, :, None]
    chosen = here[None] & ranked & hit[:, None, :]
    select = chosen.astype(jnp.bfloat16).reshape(GROUP * NZ * CAP, NZ * tokens)
    gated = jnp.where(chosen, gate[:, None, :], 0.0).reshape(GROUP * NZ * CAP, NZ * tokens)
    return select, gated


def per_device(
    patches,
    norm1_gain,
    qkv_weight,
    qkv_bias,
    out_weight,
    out_bias,
    norm2_gain,
    proj_weight,
    moe_gain,
    expert_in,
    expert_out,
    shared_in,
    shared_out,
    routes,
    gates,
):
    tile_id = lax.axis_index("tile")
    row_count = patches.shape[1]
    columns = patches.shape[2]
    width_vit = patches.shape[3]
    local_rows = row_count * columns
    tokens = local_rows // 4
    top = routes.shape[-1]
    side_a = [(t, t + 1 - 2 * (t % 2)) for t in range(NX)]
    side_b = [(t, NX - 1 - t) for t in range(NX)]
    units = expert_out.shape[1] // 2
    gate_halves, up_halves = (
        [expert_in[0, :, which, i * units : (i + 1) * units] for i in (0, 1)] for which in (0, 1)
    )
    out_halves = [expert_out[0, i * units : (i + 1) * units] for i in (0, 1)]

    def swap(halves, after):
        first, second, after = lax.optimization_barrier((halves[0], halves[1], after))
        from_a = lax.ppermute(first, "tile", side_a)
        from_b = lax.ppermute(second, "tile", side_b)
        return from_a, from_b, after

    project = lax.all_gather(proj_weight, "expert", axis=0, tiled=True)

    inputs = patches.reshape(local_rows, width_vit).astype(jnp.float32)
    normed = layer_norm(inputs, norm1_gain).astype(jnp.bfloat16)
    own_routes = lax.dynamic_index_in_dim(
        routes.reshape(NX, tokens, top), tile_id, 0, keepdims=False
    )
    table = jnp.zeros((16, 128), jnp.float32)
    table = table.at[:top, :tokens].set(own_routes.T.astype(jnp.float32))
    table = table.at[8 : 8 + top, :tokens].set(gates.reshape(tokens, top).T)
    piece, tables_z = ring_gather([("x", normed, 32), ("z", table, 16)], 0)
    out_a, out_b, piece = swap(out_halves, piece)
    piece = piece.reshape(NX * local_rows, width_vit)

    heads_here = qkv_weight.shape[2] // HD
    qkv_flat = qkv_weight.reshape(width_vit, -1)
    bias_rows = qkv_bias.reshape(1, 3, heads_here, HD)
    mixed_flat = jnp.dot(piece, qkv_flat, preferred_element_type=jnp.float32)
    mixed = (
        mixed_flat.reshape(
            piece.shape[0], 3, heads_here, HD
        )
        + bias_rows
    )
    tables = rope_tables(jnp.arange(piece.shape[0]), columns, HD)
    attended = attend(
        rotate(mixed[:, 0], tables).astype(jnp.bfloat16),
        rotate(mixed[:, 1], tables).astype(jnp.bfloat16),
        mixed[:, 2].astype(jnp.bfloat16),
        math.sqrt(HD),
    )
    partial_rows = (
        jnp.dot(attended, out_weight, preferred_element_type=jnp.float32)
        .astype(jnp.bfloat16)
        .reshape(NX, local_rows, width_vit)
    )
    (mixed_heads,) = ring_reduce([("x", partial_rows, 32, jnp.float32)], 1)
    hidden = inputs + mixed_heads + out_bias
    normed_out = layer_norm(hidden, norm2_gain).astype(jnp.bfloat16)
    merged = (
        normed_out.reshape(row_count // 2, 2, columns // 2, 2, width_vit)
        .transpose(0, 2, 1, 3, 4)
        .reshape(tokens, 4 * width_vit)
    )
    (group_merged,) = ring_gather([("x", merged, 16)], 2)
    gate_a, gate_b, group_merged = swap(gate_halves, group_merged)
    select, gated = slot_tables(tables_z, tokens, top)
    projected = jnp.dot(
        group_merged.reshape(NX * tokens, -1), project, preferred_element_type=jnp.float32
    ).astype(jnp.bfloat16)
    (pieces,) = ring_gather([("x", projected, 32)], 3)
    up_a, up_b, pieces = swap(up_halves, pieces)
    page_tokens = pieces.transpose(1, 0, 2).reshape(NX * tokens, -1)
    width_moe = page_tokens.shape[1]
    page_in = rms_norm(page_tokens.astype(jnp.float32), moe_gain).astype(jnp.bfloat16)
    tokens_moe = lax.dynamic_slice_in_dim(page_tokens, tile_id * tokens, tokens, 0)
    moe_in = lax.dynamic_slice_in_dim(page_in, tile_id * tokens, tokens, 0)

    shared_gated = jnp.dot(
        page_in, shared_in.reshape(width_moe, -1), preferred_element_type=jnp.float32
    ).reshape(NX * tokens, 2, -1)
    shared_hidden = (jax.nn.silu(shared_gated[:, 0]) * shared_gated[:, 1]).astype(jnp.bfloat16)
    shared_rows = (
        jnp.dot(shared_hidden, shared_out, preferred_element_type=jnp.float32)
        .astype(jnp.bfloat16)
        .reshape(NX, tokens, width_moe)
    )

    arrived, shared_part = dispatch(moe_in, select, shared_rows, 4)
    slots = GROUP * NZ * CAP
    arrived = arrived.reshape(3 * slots, width_moe)

    def feed_forward(rows, halves):
        hidden_rows = []
        for gate_piece, up_piece, _ in halves:
            gate_rows = jnp.dot(rows, gate_piece, preferred_element_type=jnp.float32)
            up_rows = jnp.dot(rows, up_piece, preferred_element_type=jnp.float32)
            hidden_rows.append((jax.nn.silu(gate_rows) * up_rows).astype(jnp.bfloat16))
        total = jnp.dot(
            jnp.concatenate(hidden_rows, axis=1),
            jnp.concatenate([out_piece for _, _, out_piece in halves]),
            preferred_element_type=jnp.float32,
        )
        return total.astype(jnp.bfloat16).reshape(2, GROUP, NZ * CAP, width_moe)

    second = feed_forward(
        arrived[slots:], [(gate_halves[0], up_halves[0], out_halves[0]), (gate_a, up_a, out_a)]
    )
    first = feed_forward(
        arrived[: 2 * slots], [(gate_halves[1], up_halves[1], out_halves[1]), (gate_b, up_b, out_b)]
    )
    routed = give_back(first, second, gated, tokens, 5)
    output = tokens_moe.astype(jnp.float32) + shared_part + routed
    return output.astype(jnp.bfloat16).reshape(1, row_count // 2, columns // 2, width_moe)


def solution(mesh):
    placed = (
        P("expert", "tile", None, None),
        P(),
        P(None, None, "tile"),
        P(None, "tile"),
        P("tile", None),
        P(),
        P(),
        P("expert", "tile"),
        P(),
        P("expert", None, None, "tile"),
        P("expert", "tile", None),
        P(None, None, "tile"),
        P("tile", None),
        P("expert", None, None, None),
        P("expert", "tile", None, None),
    )
    return jax.shard_map(
        per_device,
        mesh=mesh,
        in_specs=placed,
        out_specs=P("expert", "tile", None, None),
        check_vma=False,
    )
```

profile of v0, /device:TPU:8, one launch (start us, length us, event | category | flops | bytes accessed | tf_op | source)
XLA Modules:
  0.0 297.7 jit_solution(6196265210840032722)
XLA Ops:
  6.5 0.7 all-gather.2.cloned.1.call-update
  7.3 0.9 reshape.431
  8.2 0.8 reshape.432
  9.0 1.1 convert_reduce_fusion
  10.1 0.1 div.108
  10.2 1.2 fusion.21
  11.4 0.1 rsqrt.28
  11.5 0.4 scatter.9.refs_1_
  11.9 1.9 fusion.24.refs_0_
  13.8 23.7 %shard_map.145 = (bf16[4,128,1152]{2,1,0:T(8,128)(2,1)}, f32[8,16,128]{2,1,0:T(8,128)}) custom-call(bf16[128,1152]{1,0:T(8,128)(2,1)} %fusion.24.refs_0_, f32[16,128]{1,0:T(8,128)} %copy-done.13), custom_call_target="tpu_custom_call" | custom-call | tf_op jit(solution)/shard_map/pallas_call | solution.py:178
  37.5 2.6 slice_bitcast_fusion
  40.1 0.1 add.187
  40.2 0.4 multiply_cosine_fusion.1
  40.6 3.3 %convolution_add_fusion = f32[512,3,4,72]{0,3,2,1:T(8,128)S(1)} fusion(bf16[512,1152,1,1]{1,0,3,2:T(8,128)(2,1)} %bitcast.171, bf16[3,4,72,1152]{3,2,1,0:T(8,128)(2,1)} %bitcast.170, f32[3,4,72]{2,1,0:T(4,128)S(1)} %add.187), kind=kOutput, calls=%fused_computation.13 | convolution fusion | flops 1019658240 | bytes 4943232 | tf_op jit(solution)/shard_map/dot_general | solution.py:691
  43.9 0.1 slice_bitcast_fusion.7
  44.0 0.1 subtract_convert_fusion.3
  44.2 1.0 subtract_convert_fusion.1
  45.2 4.5 %fusion.82 = (f32[4,512]{1,0:T(4,128)S(1)}, f32[4,512,512]{1,2,0:T(8,128)}) fusion(bf16[512,4,18]{0,2,1:T(8,128)(2,1)} %get-tuple-element.75, bf16[512,4,18]{0,2,1:T(8,128)(2,1)} %get-tuple-element.76, bf16[512,4,18]{0,2,1:T(8,128)(2,1)S(1)} %get-tuple-element.70, bf16[512,4,18]{0,2,1:T(8,128)(2,1)S(1)} %get-tuple-element.69, ...), kind=kOutput, calls=%fused_computation.157 | convolution fusion | flops 156500480 | bytes 4792320 | tf_op jit(solution)/shard_map/sub | solution.py:64
  49.7 2.9 fusion.14
  52.7 1.9 convolution_convert_fusion.2
  54.6 12.5 %shard_map.146 = f32[128,1152]{1,0:T(8,128)} custom-call(bf16[4,128,1152]{2,1,0:T(8,128)(2,1)} %bitcast.165), custom_call_target="tpu_custom_call" | custom-call | tf_op jit(solution)/shard_map/pallas_call | solution.py:274
  67.1 1.2 fusion.48
  68.4 1.3 multiply_reduce_fusion.1
  69.7 1.2 multiply_convert_fusion
  70.9 0.1 reshape.437
  71.0 0.2 copy.45
  71.2 0.9 reshape.438.refs_0_
  72.1 12.3 %shard_map.147 = bf16[4,32,4608]{2,1,0:T(8,128)(2,1)} custom-call(bf16[32,4608]{1,0:T(8,128)(2,1)} %reshape.438.refs_0_), custom_call_target="tpu_custom_call" | custom-call | tf_op jit(solution)/shard_map/pallas_call | solution.py:178
  84.4 3.5 %slice_bitcast_fusion.2 = (bf16[2048,176]{0,1:T(8,128)(2,1)}, bf16[2048,176]{0,1:T(8,128)(2,1)}, bf16[2048,176]{0,1:T(8,128)(2,1)}, bf16[2048,176]{0,1:T(8,128)(2,1)}) fusion(bf16[1,2048,2,352]{1,3,2,0:T(8,128)(2,1)} %param.28), kind=kLoop, calls=%fused_computation.33 | loop fusion | bytes 5767168 | tf_op jit(solution)/shard_map/squeeze | solution.py:664
  87.9 1.4 collective-permute-start.3
  89.3 0.6 collective-permute-start.5
  89.9 2.6 collective-permute-start
  92.5 0.6 collective-permute-start.2
  93.3 0.1 eq.87
  93.5 0.1 compare_reduce_fusion
  93.6 0.2 fusion.44
  93.9 0.8 fusion.36.select_ref
  94.8 0.9 bitcast_select_fusion.gated_ref
  95.7 4.1 %convolution_convert_fusion.4.refs_0_ = bf16[128,512]{1,0:T(8,128)(2,1)} fusion(bf16[128,4608]{1,0:T(8,128)(2,1)} %bitcast.152, bf16[4608,512]{1,0:T(8,128)(2,1)} %all-gather.2.cloned.1.call-done), kind=kOutput, calls=%fused_computation.27 | convolution fusion | flops 604045312 | bytes 6029312 | tf_op jit(solution)/shard_map/dot_general | solution.py:721
  99.8 25.4 %shard_map.148 = bf16[4,128,512]{2,1,0:T(8,128)(2,1)} custom-call(bf16[128,512]{1,0:T(8,128)(2,1)} %convolution_convert_fusion.4.refs_0_), custom_call_target="tpu_custom_call" | custom-call | tf_op jit(solution)/shard_map/pallas_call | solution.py:178
  125.2 1.3 fusion.17
  126.5 2.0 fusion.19
  128.6 2.0 copy.32
  130.8 2.2 fusion.4
  133.0 1.3 convolution_convert_fusion.3
  134.3 0.8 fusion.42.rows_ref
  135.1 64.3 %shard_map.149 = (bf16[3,8,48,2048]{3,2,1,0:T(8,128)(2,1)}, f32[32,2048]{1,0:T(8,128)}) custom-call(bf16[32,2048]{1,0:T(8,128)(2,1)} %fusion.42.rows_ref, bf16[384,256]{1,0:T(8,128)(2,1)} %fusion.36.select_ref, bf16[4,32,2048]{2,1,0:T(8,128)(2,1)} %bitcast.164), custom_call_target="tpu_custom_call" | custom-call | tf_op jit(solution)/shard_map/pallas_call | solution.py:459
  199.4 3.6 %fusion.81 = (bf16[2,8,48,2048]{3,2,1,0:T(8,128)(2,1)S(1)}, bf16[2,8,48,2048]{3,2,1,0:T(8,128)(2,1)S(1)}) fusion(bf16[3,8,48,2048]{3,2,1,0:T(8,128)(2,1)} %get-tuple-element.48), kind=kLoop, calls=%fused_computation.156 | loop fusion | bytes 12582912 | tf_op jit(solution)/shard_map/slice | solution.py:760
  202.9 0.1 copy-done.3
  203.0 1.2 fusion.79
  204.2 0.1 collective-permute-start.4
  204.3 1.2 fusion.80
  205.5 1.2 fusion.16
  206.8 2.3 collective-permute-start.1
  209.1 2.3 fusion.84
  211.4 1.2 fusion.15
  212.6 2.3 fusion.83
  214.9 3.3 %collective-permute-done.4 = bf16[2048,176]{0,1:T(8,128)(2,1)S(1)} collective-permute-done((bf16[2048,176]{0,1:T(8,128)(2,1)S(1)}, bf16[2048,176]{0,1:T(8,128)(2,1)S(1)}, u32[]{:S(2)}, u32[]{:S(2)}) %collective-permute-start.4) | collective-permute-done | bytes 720928 | tf_op jit(solution)/shard_map/ppermute | solution.py:670
  218.2 1.2 multiply_convert_fusion.1
  219.4 4.8 %convolution_convert_fusion = bf16[768,2048]{1,0:T(8,128)(2,1)} fusion(bf16[176,2048]{1,0:T(8,128)(2,1)} %collective-permute-done.5, bf16[176,2048]{1,0:T(8,128)(2,1)} %get-tuple-element.54, bf16[768,176]{0,1:T(8,128)(2,1)S(1)} %multiply_convert_fusion.1, bf16[768,176]{0,1:T(8,128)(2,1)S(1)} %fusion.16), kind=kOutput, calls=%fused_computation.5 | convolution fusion | flops 1112834048 | bytes 5128192 | tf_op jit(solution)/shard_map/dot_general | solution.py:752
  224.2 1.3 multiply_convert_fusion.2
  225.5 4.8 %convolution_convert_fusion.1 = bf16[768,2048]{1,0:T(8,128)(2,1)} fusion(bf16[176,2048]{1,0:T(8,128)(2,1)} %collective-permute-done.2, bf16[176,2048]{1,0:T(8,128)(2,1)} %get-tuple-element.51, bf16[768,176]{0,1:T(8,128)(2,1)S(1)} %multiply_convert_fusion.2, bf16[768,176]{0,1:T(8,128)(2,1)S(1)} %fusion.15), kind=kOutput, calls=%fused_computation.6 | convolution fusion | flops 1112834048 | bytes 5128192 | tf_op jit(solution)/shard_map/dot_general | solution.py:752
  230.3 58.8 %shard_map.150 = f32[32,2048]{1,0:T(8,128)} custom-call(bf16[2,8,48,2048]{3,2,1,0:T(8,128)(2,1)} %bitcast.154, bf16[2,8,48,2048]{3,2,1,0:T(8,128)(2,1)} %bitcast.153, f32[384,256]{1,0:T(8,128)} %bitcast_select_fusion.gated_ref), custom_call_target="tpu_custom_call" | custom-call | tf_op jit(solution)/shard_map/pallas_call | solution.py:591
  289.2 1.7 fusion.40
  (64 shorter events, 0.6 us)
Async XLA Ops:
  6.5 124.2 %copy-start = (bf16[2048,2,352]{0,2,1:T(8,128)(2,1)S(1)}, bf16[2048,2,352]{0,2,1:T(8,128)(2,1)}, u32[]{:S(2)}) copy-start(bf16[2048,2,352]{0,2,1:T(8,128)(2,1)} %param.30) | copy-start | bytes 8650756
  6.5 33.6 %copy-start.15 = (f32[3,288]{1,0:T(4,128)S(1)}, f32[3,288]{1,0:T(4,128)}, u32[]{:S(2)}) copy-start(f32[3,288]{1,0:T(4,128)} %param.22) | copy-start | bytes 10372
  6.5 89.2 %all-gather.2.cloned.1.call-start = ((), (), s32[]{:S(2)}) async-start(), calls=%async_computation | async-start | bytes 4792320 | tf_op jit(solution)/shard_map/all_gather | solution.py:674
  11.9 1.9 copy-start.13
  43.9 1.3 copy-start.6
  49.7 3.0 copy-start.16
  52.6 14.5 %copy-start.1 = (bf16[1,4,32,1152]{3,2,1,0:T(8,128)(2,1)S(1)}, bf16[1,4,32,1152]{3,2,1,0:T(8,128)(2,1)}, u32[]{:S(2)}) copy-start(bf16[1,4,32,1152]{3,2,1,0:T(8,128)(2,1)} %param.19) | copy-start | bytes 884740
  52.6 14.5 %copy-start.10 = (f32[1152]{0:T(1024)S(1)}, f32[1152]{0:T(1024)}, u32[]{:S(2)}) copy-start(f32[1152]{0:T(1024)} %param.24) | copy-start | bytes 13828
  52.6 17.0 %copy-start.14 = (f32[1152]{0:T(1024)S(1)}, f32[1152]{0:T(1024)}, u32[]{:S(2)}) copy-start(f32[1152]{0:T(1024)} %param.25) | copy-start | bytes 13828
  84.4 8.8 %copy-start.12 = (f32[2048]{0:T(1024)S(1)}, f32[2048]{0:T(1024)}, u32[]{:S(2)}) copy-start(f32[2048]{0:T(1024)} %param.27) | copy-start | bytes 24580
  84.4 8.8 %copy-start.11 = (f32[8,16,128]{2,1,0:T(8,128)S(1)}, f32[8,16,128]{2,1,0:T(8,128)}, u32[]{:S(2)}) copy-start(f32[8,16,128]{2,1,0:T(8,128)} %get-tuple-element.46) | copy-start | bytes 196612
  87.9 118.8 %collective-permute-start.3 = (bf16[2048,176]{0,1:T(8,128)(2,1)}, bf16[2048,176]{0,1:T(8,128)(2,1)}, u32[]{:S(2)}, u32[]{:S(2)}) collective-permute-start(bf16[2048,176]{0,1:T(8,128)(2,1)} %get-tuple-element.52), channel_id=1, source_target_pairs={{0,64},{64,0},{128,192},{192,128},{1,65},{65,1},{129,193},{193,129... | collective-permute-start | bytes 2162696 | tf_op jit(solution)/shard_map/ppermute | solution.py:670
  89.3 130.1 %collective-permute-start.5 = (bf16[176,2048]{1,0:T(8,128)(2,1)}, bf16[176,2048]{1,0:T(8,128)(2,1)}, u32[]{:S(2)}, u32[]{:S(2)}) collective-permute-start(bf16[176,2048]{1,0:T(8,128)(2,1)} %get-tuple-element.54), channel_id=1, source_target_pairs={{0,64},{64,0},{128,192},{192,128},{1,65},{65,1},{129,193},{193,129... | collective-permute-start | bytes 2162696 | tf_op jit(solution)/shard_map/ppermute | solution.py:670
  89.9 122.7 %collective-permute-start = (bf16[2048,176]{0,1:T(8,128)(2,1)}, bf16[2048,176]{0,1:T(8,128)(2,1)}, u32[]{:S(2)}, u32[]{:S(2)}) collective-permute-start(bf16[2048,176]{0,1:T(8,128)(2,1)} %get-tuple-element.49), channel_id=1, source_target_pairs={{0,192},{64,128},{128,64},{192,0},{1,193},{65,129},{129,65},{193,1... | collective-permute-start | bytes 2162696 | tf_op jit(solution)/shard_map/ppermute | solution.py:671
  92.5 132.9 %collective-permute-start.2 = (bf16[176,2048]{1,0:T(8,128)(2,1)}, bf16[176,2048]{1,0:T(8,128)(2,1)}, u32[]{:S(2)}, u32[]{:S(2)}) collective-permute-start(bf16[176,2048]{1,0:T(8,128)(2,1)} %get-tuple-element.51), channel_id=1, source_target_pairs={{0,192},{64,128},{128,64},{192,0},{1,193},{65,129},{129,65},{193,1... | collective-permute-start | bytes 2162696 | tf_op jit(solution)/shard_map/ppermute | solution.py:671
  125.2 5.4 %copy-start.2 = (bf16[4,128,512]{2,1,0:T(8,128)(2,1)S(1)}, bf16[4,128,512]{2,1,0:T(8,128)(2,1)}, u32[]{:S(2)}) copy-start(bf16[4,128,512]{2,1,0:T(8,128)(2,1)} %shard_map.148) | copy-start | bytes 1572868
  130.6 2.4 copy-start.4
  130.7 3.6 %copy-start.5 = (bf16[4,16,8,512]{3,2,0,1:T(8,128)(2,1)}, bf16[4,16,8,512]{3,2,0,1:T(8,128)(2,1)S(1)}, u32[]{:S(2)}) copy-start(bf16[4,16,8,512]{3,2,0,1:T(8,128)(2,1)S(1)} %copy.40) | copy-start | bytes 1572868
  199.3 3.7 %copy-start.3 = (bf16[1,2048,2,352]{1,3,2,0:T(8,128)(2,1)S(1)}, bf16[1,2048,2,352]{1,3,2,0:T(8,128)(2,1)}, u32[]{:S(2)}) copy-start(bf16[1,2048,2,352]{1,3,2,0:T(8,128)(2,1)} %param.28) | copy-start | bytes 8650756
  203.0 1.2 copy-start.8
  204.2 13.9 %collective-permute-start.4 = (bf16[2048,176]{0,1:T(8,128)(2,1)S(1)}, bf16[2048,176]{0,1:T(8,128)(2,1)S(1)}, u32[]{:S(2)}, u32[]{:S(2)}) collective-permute-start(bf16[2048,176]{0,1:T(8,128)(2,1)S(1)} %copy-done.8), channel_id=1, source_target_pairs={{0,64},{64,0},{128,192},{192,128},{1,65},{65,1},{129,193},{193,129... | collective-permute-start | bytes 2162696 | tf_op jit(solution)/shard_map/ppermute | solution.py:670
  205.5 1.2 copy-start.7
  206.8 17.4 %collective-permute-start.1 = (bf16[2048,176]{0,1:T(8,128)(2,1)S(1)}, bf16[2048,176]{0,1:T(8,128)(2,1)S(1)}, u32[]{:S(2)}, u32[]{:S(2)}) collective-permute-start(bf16[2048,176]{0,1:T(8,128)(2,1)S(1)} %copy-done.7), channel_id=1, source_target_pairs={{0,192},{64,128},{128,64},{192,0},{1,193},{65,129},{129,65},{193,1... | collective-permute-start | bytes 2162696 | tf_op jit(solution)/shard_map/ppermute | solution.py:671
  230.3 58.9 %copy-start.9 = (f32[32,2048]{1,0:T(8,128)S(1)}, f32[32,2048]{1,0:T(8,128)}, u32[]{:S(2)}) copy-start(f32[32,2048]{1,0:T(8,128)} %get-tuple-element.47) | copy-start | bytes 786436
Sparse Core Ops, SparseCore 0:
  10.1 80.7 all-gather.1
where the time goes:
time: 299 us; the launch traced here: 298 us
  Pallas kernels  197 us (66%)
  matrix products  42 us (14%)
  other arithmetic  17.3 us (6%)
  local copies, waits for them, and re-layouts  15.9 us (5%)
  between operations  13.8 us (5%)
  starting transfers between devices  7.67 us (3%)
  waiting for transfers between devices  3.99 us (1%)
    pallas_call x1, Pallas kernels, dispatch(): pl.pallas_call(dispatch_kernel, out_shape=[jax.ShapeDtypeStruct((3, GROUP...  64.3 us
    pallas_call x3, Pallas kernels, ring_gather(): pl.pallas_call(kernel, out_shape=[jax.ShapeDtypeStruct((sizes[axis],) + b...  61.3 us
    pallas_call x1, Pallas kernels, give_back(): pl.pallas_call(give_back_kernel, out_shape=jax.ShapeDtypeStruct((tokens,...  58.8 us
    pallas_call x1, Pallas kernels, ring_reduce(): pl.pallas_call(kernel, out_shape=[jax.ShapeDtypeStruct(block.shape[1:], k...  12.5 us
    dot_general x2, matrix products, feed_forward(): jnp.dot(jnp.concatenate(hidden_rows, axis=1), jnp.concatenate([out_piece...  9.63 us
    dot_general x4, matrix products, feed_forward(): gate_rows = jnp.dot(rows, gate_piece, preferred_element_type=jnp.float32)  6.99 us
  transfers between devices with their start and end apart: 7, of which 1 were waited for; matrix products, arithmetic and copies ran while one was open for 23% of the time, Pallas kernels for 46%

commit v1 on v0

--- a/solution.py
+++ b/solution.py
@@ -22,12 +22,6 @@
     centre = values - jnp.mean(values, axis=-1, keepdims=True)
     spread = jnp.mean(centre * centre, axis=-1, keepdims=True)
     return centre * lax.rsqrt(spread + norm_eps) * gain_vec
-
-
-def rms_norm(values, gain_vec):
-    return (
-        values * lax.rsqrt(jnp.mean(values * values, axis=-1, keepdims=True) + norm_eps) * gain_vec
-    )
 
 
 def rope_tables(positions, columns, head_size):
@@ -331,15 +325,43 @@
 X_COPIES = sum(length for _, _, length in X_STREAMS)
 
 
-def dispatch_kernel(
-    rows_ref, select_ref, shared_ref, out_ref, sum_ref, ring_ref, chosen_ref, land_ref, stage_ref,
-    send_sem, recv_sem, local_sem,
+PER_JOB = GROUP // 2
+
+
+def expert_kernel(
+    rows_ref, select_ref, shared_ref, gated_ref, tokens_ref, in_ref, down_ref,
+    gate_a_ref, up_a_ref, down_a_ref, gate_b_ref, up_b_ref, down_b_ref,
+    out_ref,
+    ring_ref, chosen_ref, sum_land_ref, sum_stage_ref, slots_ref, weight_ref, hidden_ref, part_ref,
+    high_ref, low_ref, side_ref, stage_ref, back_ref, mix_ref, land_ref, step_ref, base_ref,
+    send_sem, recv_sem, local_sem, weight_sem, side_send, side_recv,
 ):
     tile, z, me, across, group, ring = places()
     tokens, width = rows_ref.shape
     chunk, half_rows = width // CHUNKS, tokens // 2
+    slots = NZ * CAP
+    units = down_a_ref.shape[0]
     post = Sender(send_sem, recv_sem)
     peers = [(me + k) % GROUP for k in range(1, GROUP)]
+    low_units, high_units = pl.ds(0, units), pl.ds(units, units)
+    loads = []
+    for where, source in (
+        ((0, 0, 0), in_ref.at[0, high_units]),
+        ((0, 0, 1), in_ref.at[1, high_units]),
+        ((0, 0, 2), down_ref.at[high_units]),
+        ((0, 1, 0), gate_b_ref),
+        ((0, 1, 1), up_b_ref),
+        ((0, 1, 2), down_b_ref),
+        ((1, 0, 0), in_ref.at[0, low_units]),
+        ((1, 0, 1), in_ref.at[1, low_units]),
+        ((1, 0, 2), down_ref.at[low_units]),
+        ((1, 1, 0), gate_a_ref),
+        ((1, 1, 1), up_a_ref),
+        ((1, 1, 2), down_a_ref),
+    ):
+        copy = pltpu.make_async_copy(source, weight_ref.at[where], weight_sem.at[len(loads)])
+        copy.start()
+        loads.append(copy)
     greet(
         [ring((z + 1) % NZ), ring((z + NZ - 1) % NZ)]
         + [group(peer) for peer in peers]
@@ -379,26 +401,27 @@
             else:
                 copy, before = sums[(sign, half, step - 1)]
                 copy.wait_recv()
-                stage_ref[slot] = (
+                sum_stage_ref[slot] = (
                     shared_ref[target, part[half]].astype(jnp.float32)
-                    + land_ref[before].astype(jnp.float32)
-                ).astype(stage_ref.dtype)
-                source = stage_ref.at[slot]
-            copy = post.send(source, land_ref.at[slot], {"tile": (tile + sign + NX) % NX})
+                    + sum_land_ref[before].astype(jnp.float32)
+                ).astype(sum_stage_ref.dtype)
+                source = sum_stage_ref.at[slot]
+            copy = post.send(source, sum_land_ref.at[slot], {"tile": (tile + sign + NX) % NX})
             sums[(sign, half, step)] = (copy, slot)
 
     shared_step(0)
     for j in range(CHUNKS):
         ring_ref[j, z] = rows_ref[:, j * chunk : (j + 1) * chunk]
-
-    swaps, own = {}, []
-
-    def hand_on(j, member, source):
+    gated = gated_ref[...].T
+    high = gated.astype(high_ref.dtype)
+    high_ref[...] = high
+    low_ref[...] = (gated - high.astype(jnp.float32)).astype(low_ref.dtype)
+
+    swaps, own, handed = {}, [], []
+
+    def hand_on(j, k, source):
         for side in (0, 1):
-            post_to = out_ref.at[2 * side, member, :, cols[j]]
-            handed.append(post.send(source, post_to, across[side]))
-
-    handed = []
+            handed.append(post.send(source, slots_ref.at[2 * side, k, :, cols[j]], across[side]))
 
     def choose(j):
         for sign, half, _ in Z_STREAMS:
@@ -409,120 +432,122 @@
             .astype(chosen_ref.dtype)
             .reshape(chosen_ref.shape[1:])
         )
-        for k, peer in enumerate(peers):
+        for k, peer in enumerate(peers, 1):
             swaps[(j, k)] = post.send(
-                chosen_ref.at[j, peer], out_ref.at[1, me, :, cols[j]], group(peer)
+                chosen_ref.at[j, peer], slots_ref.at[1, k, :, cols[j]], group(peer)
             )
         copy = pltpu.make_async_copy(
-            chosen_ref.at[j, me], out_ref.at[1, me, :, cols[j]], local_sem.at[j]
+            chosen_ref.at[j, me], slots_ref.at[1, 0, :, cols[j]], local_sem.at[j]
         )
         copy.start()
         own.append(copy)
-        hand_on(j, me, chosen_ref.at[j, me])
+        hand_on(j, 0, chosen_ref.at[j, me])
+
+    def forward(j):
+        for k in range(1, GROUP):
+            swaps[(j, k)].wait_recv()
+            hand_on(j, k, slots_ref.at[1, k, :, cols[j]])
 
     for wave in range(CHUNKS + Z_HALF - 1):
         for number in range(Z_HALF, 1, -1):
             j = wave - (number - 2)
             if 0 <= j < CHUNKS:
                 hop(j, number)
-        j = wave - (Z_HALF - 1)
         if wave == 0:
             shared_step(1)
+        j = wave - (Z_HALF - 1)
         if 0 <= j < CHUNKS:
             choose(j)
-    for j in range(CHUNKS):
-        for k in range(GROUP - 1):
-            swaps[(j, k)].wait_recv()
-            source = (me - 1 - k + GROUP) % GROUP
-            hand_on(j, source, out_ref.at[1, source, :, cols[j]])
+        if 0 <= j - 2 < CHUNKS:
+            forward(j - 2)
+    for j in range(CHUNKS - 2, CHUNKS):
+        forward(j)
+
+    def feed_forward(which, mine, job):
+        first = job * PER_JOB
+        place = 2 * which * (1 - mine) + mine
+        rows = slots_ref[place, pl.ds(first, PER_JOB)].reshape(PER_JOB * slots, width)
+        contract = (((1,), (1,)), ((), ()))
+        for piece in (0, 1):
+            gate = lax.dot_general(
+                rows, weight_ref[which, piece, 0], contract, preferred_element_type=jnp.float32
+            )
+            up = lax.dot_general(
+                rows, weight_ref[which, piece, 1], contract, preferred_element_type=jnp.float32
+            )
+            hidden_ref[piece] = (gate / (1.0 + jnp.exp(-gate)) * up).astype(hidden_ref.dtype)
+        for j in range(CHUNKS):
+            total = jnp.dot(
+                hidden_ref[0], weight_ref[which, 0, 2, :, cols[j]],
+                preferred_element_type=jnp.float32,
+            ) + jnp.dot(
+                hidden_ref[1], weight_ref[which, 1, 2, :, cols[j]],
+                preferred_element_type=jnp.float32,
+            )
+            part_ref[which, mine, pl.ds(first, PER_JOB), :, cols[j]] = total.astype(
+                part_ref.dtype
+            ).reshape(PER_JOB, slots, chunk)
+
+    def side_copy(which, j, k):
+        number = (which * CHUNKS + j) * GROUP + k
+        neighbour = tile + 1 - 2 * (tile % 2)
+        other = NX - 1 - tile
+        return pltpu.make_async_remote_copy(
+            src_ref=part_ref.at[which, 0, k, :, cols[j]],
+            dst_ref=side_ref.at[which, j, k],
+            send_sem=side_send.at[number],
+            recv_sem=side_recv.at[number],
+            device_id={"tile": neighbour + which * (other - neighbour)},
+            device_id_type=MESH,
+        )
+
+    for copy in loads + own:
+        copy.wait()
+
+    def own_job(i, carry):
+        feed_forward(i % 2, 1, i // 2)
+        return carry
+
+    lax.fori_loop(0, 4, own_job, 0)
+    for copy in handed:
+        copy.wait_recv()
+
+    def side_job(i, carry):
+        which, job = i % 2, i // 2
+        feed_forward(which, 0, job)
+        for j in range(CHUNKS):
+            for k in range(PER_JOB):
+                side_copy(which, j, job * PER_JOB + k).start()
+        return carry
+
+    lax.fori_loop(0, 4, side_job, 0)
+
     for half in (0, 1):
         total = shared_ref[tile, part[half]].astype(jnp.float32)
         for sign, this, length in X_STREAMS:
             if this == half:
                 copy, slot = sums[(sign, half, length - 1)]
                 copy.wait_recv()
-                total = total + land_ref[slot].astype(jnp.float32)
-        sum_ref[part[half]] = total
-    for copy in handed:
-        copy.wait_recv()
-    for copy in post.made:
-        copy.wait_send()
-    for copy in own:
-        copy.wait()
-
-
-def dispatch(rows, select, shared_rows, collective_id):
-    tokens, width = rows.shape
-    slots = NZ * CAP
-    chunk = width // CHUNKS
-    copies = CHUNKS * (Z_COPIES + (GROUP - 1) + 2 * GROUP) + X_COPIES
-    return pl.pallas_call(
-        dispatch_kernel,
-        out_shape=[
-            jax.ShapeDtypeStruct((3, GROUP, slots, width), rows.dtype),
-            jax.ShapeDtypeStruct((tokens, width), jnp.float32),
-        ],
-        in_specs=[pl.BlockSpec(memory_space=pltpu.VMEM)] * 3,
-        out_specs=[pl.BlockSpec(memory_space=pltpu.VMEM)] * 2,
-        scratch_shapes=[
-            pltpu.VMEM((CHUNKS, NZ, tokens, chunk), rows.dtype),
-            pltpu.VMEM((CHUNKS, GROUP, slots, chunk), rows.dtype),
-            pltpu.VMEM((X_COPIES, tokens // 2, width), rows.dtype),
-            pltpu.VMEM((X_COPIES, tokens // 2, width), rows.dtype),
-            pltpu.SemaphoreType.DMA((copies,)),
-            pltpu.SemaphoreType.DMA((copies,)),
-            pltpu.SemaphoreType.DMA((CHUNKS,)),
-        ],
-        compiler_params=pltpu.CompilerParams(collective_id=collective_id, has_side_effects=True),
-    )(rows, select, shared_rows)
-
-
-def give_back_kernel(
-    first_ref, second_ref, gated_ref, out_ref, high_ref, low_ref, side_ref, stage_ref, back_ref, mix_ref,
-    land_ref, step_ref, send_sem, recv_sem,
-):
-    _, z, me, across, group, ring = places()
-    tokens, width = out_ref.shape
-    chunk, half_rows = width // CHUNKS, tokens // 2
-    post = Sender(send_sem, recv_sem)
-    peers = [(me + k) % GROUP for k in range(1, GROUP)]
-    greet(
-        [ring((z + 1) % NZ), ring((z + NZ - 1) % NZ)]
-        + [group(peer) for peer in peers]
-        + list(across)
-    )
-    cols = [pl.ds(j * chunk, chunk) for j in range(CHUNKS)]
-    part = [pl.ds(h * half_rows, half_rows) for h in (0, 1)]
-    order = peers + [me]
-    sides, swaps, steps = {}, {}, {}
-    for j in range(CHUNKS):
-        for k, member in enumerate(order):
-            for side, source in ((0, first_ref.at[0]), (1, second_ref.at[1])):
-                sides[(j, k, side)] = post.send(
-                    source.at[member, :, cols[j]], side_ref.at[side, j, member], across[side]
-                )
-
-    gated = gated_ref[...].T
-    high = gated.astype(high_ref.dtype)
-    high_ref[...] = high
-    low_ref[...] = (gated - high.astype(jnp.float32)).astype(low_ref.dtype)
-
-    def add_up(j):
-        for k, member in enumerate(order):
-            for side in (0, 1):
-                sides[(j, k, side)].wait_recv()
+                total = total + sum_land_ref[slot].astype(jnp.float32)
+        base_ref[part[half]] = total + tokens_ref[part[half]].astype(jnp.float32)
+    returns, steps = {}, {}
+
+    def add_up(j, ks):
+        for k in ks:
+            for which in (0, 1):
+                side_copy(which, j, k).wait_recv()
             total = (
-                first_ref[1, member, :, j * chunk : (j + 1) * chunk].astype(jnp.float32)
-                + second_ref[0, member, :, j * chunk : (j + 1) * chunk].astype(jnp.float32)
-                + side_ref[0, j, member].astype(jnp.float32)
-                + side_ref[1, j, member].astype(jnp.float32)
+                part_ref[0, 1, k, :, cols[j]].astype(jnp.float32)
+                + part_ref[1, 1, k, :, cols[j]].astype(jnp.float32)
+                + side_ref[0, j, k].astype(jnp.float32)
+                + side_ref[1, j, k].astype(jnp.float32)
             ).astype(stage_ref.dtype)
-            if k == GROUP - 1:
-                back_ref[j, member] = total
+            if k == 0:
+                back_ref[j, me] = total
             else:
-                stage_ref[j, member] = total
-                swaps[(j, k)] = post.send(
-                    stage_ref.at[j, member], back_ref.at[j, me], group(member)
+                stage_ref[j, k] = total
+                returns[(j, k)] = post.send(
+                    stage_ref.at[j, k], back_ref.at[j, me], group((me - k + GROUP) % GROUP)
                 )
 
     def step(j, number):
@@ -545,8 +570,8 @@
             )
 
     def combine(j):
-        for k in range(GROUP - 1):
-            swaps[(j, k)].wait_recv()
+        for k in range(1, GROUP):
+            returns[(j, k)].wait_recv()
         back = back_ref[j].reshape(high_ref.shape[1], chunk)
         mix_ref[j] = (
             (
@@ -558,55 +583,156 @@
         )
         step(j, 0)
 
-    def finish(j):
-        for half in (0, 1):
-            total = mix_ref[j, z, part[half]].astype(jnp.float32)
-            for i, (_, this, length) in enumerate(Z_STREAMS):
-                if this == half:
-                    steps[(j, i, length - 1)].wait_recv()
-                    total = total + land_ref[j, i * Z_HALF + length - 1].astype(jnp.float32)
-            out_ref[half * half_rows : (half + 1) * half_rows, j * chunk : (j + 1) * chunk] = total
-
+    for j in range(CHUNKS):
+        add_up(j, range(PER_JOB))
     for wave in range(CHUNKS + Z_HALF + 1):
         if wave < CHUNKS:
-            add_up(wave)
+            add_up(wave, range(PER_JOB, GROUP))
         if 0 <= wave - 1 < CHUNKS:
             combine(wave - 1)
         for number in range(1, Z_HALF):
             if 0 <= wave - 1 - number < CHUNKS:
                 step(wave - 1 - number, number)
     for j in range(CHUNKS):
-        finish(j)
+        for half in (0, 1):
+            total = base_ref[part[half], cols[j]] + mix_ref[j, z, part[half]].astype(
+                jnp.float32
+            )
+            for i, (_, this, length) in enumerate(Z_STREAMS):
+                if this == half:
+                    steps[(j, i, length - 1)].wait_recv()
+                    total = total + land_ref[j, i * Z_HALF + length - 1].astype(jnp.float32)
+            out_ref[part[half], cols[j]] = total.astype(out_ref.dtype)
     for copy in post.made:
         copy.wait_send()
-
-
-def give_back(first, second, gated, tokens, collective_id):
-    width = first.shape[-1]
+    for which in (0, 1):
+        for j in range(CHUNKS):
+            for k in range(GROUP):
+                side_copy(which, j, k).wait_send()
+
+
+def expert_layer(rows, select, shared_rows, gated, tokens_moe, weights, collective_id):
+    tokens, width = rows.shape
     slots = NZ * CAP
     chunk = width // CHUNKS
-    copies = CHUNKS * (2 * GROUP + (GROUP - 1) + Z_COPIES)
-    boxes = pltpu.VMEM((CHUNKS, len(Z_STREAMS) * Z_HALF, tokens // 2, chunk), first.dtype)
-    blocks = pltpu.VMEM((CHUNKS, GROUP, slots, chunk), first.dtype)
+    kind = rows.dtype
+    units = weights[-1].shape[0]
+    copies = CHUNKS * (2 * Z_COPIES + 2 * (GROUP - 1) + 2 * GROUP) + X_COPIES
+    boxes = pltpu.VMEM((CHUNKS, len(Z_STREAMS) * Z_HALF, tokens // 2, chunk), kind)
+    blocks = pltpu.VMEM((CHUNKS, GROUP, slots, chunk), kind)
+    shared_boxes = pltpu.VMEM((X_COPIES, tokens // 2, width), kind)
+    spread = pltpu.VMEM((CHUNKS, NZ, tokens, chunk), kind)
     return pl.pallas_call(
-        give_back_kernel,
-        out_shape=jax.ShapeDtypeStruct((tokens, width), jnp.float32),
-        in_specs=[pl.BlockSpec(memory_space=pltpu.VMEM)] * 3,
+        expert_kernel,
+        out_shape=jax.ShapeDtypeStruct((tokens, width), kind),
+        in_specs=[pl.BlockSpec(memory_space=pltpu.VMEM)] * 5
+        + [pl.BlockSpec(memory_space=pl.ANY)] * len(weights),
         out_specs=pl.BlockSpec(memory_space=pltpu.VMEM),
         scratch_shapes=[
-            pltpu.VMEM(gated.shape[::-1], first.dtype),
-            pltpu.VMEM(gated.shape[::-1], first.dtype),
-            pltpu.VMEM((2, CHUNKS, GROUP, slots, chunk), first.dtype),
+            spread,
+            blocks,
+            shared_boxes,
+            shared_boxes,
+            pltpu.VMEM((3, GROUP, slots, width), kind),
+            pltpu.VMEM((2, 2, 3, units, width), kind),
+            pltpu.VMEM((2, PER_JOB * slots, units), kind),
+            pltpu.VMEM((2, 2, GROUP, slots, width), kind),
+            pltpu.VMEM(gated.shape[::-1], kind),
+            pltpu.VMEM(gated.shape[::-1], kind),
+            pltpu.VMEM((2, CHUNKS, GROUP, slots, chunk), kind),
             blocks,
             blocks,
-            pltpu.VMEM((CHUNKS, NZ, tokens, chunk), first.dtype),
+            spread,
             boxes,
             boxes,
+            pltpu.VMEM((tokens, width), jnp.float32),
             pltpu.SemaphoreType.DMA((copies,)),
             pltpu.SemaphoreType.DMA((copies,)),
+            pltpu.SemaphoreType.DMA((CHUNKS,)),
+            pltpu.SemaphoreType.DMA((12,)),
+            pltpu.SemaphoreType.DMA((2 * CHUNKS * GROUP,)),
+            pltpu.SemaphoreType.DMA((2 * CHUNKS * GROUP,)),
+        ],
+        compiler_params=pltpu.CompilerParams(
+            collective_id=collective_id, has_side_effects=True, vmem_limit_bytes=56 * 2**20
+        ),
+    )(rows, select, shared_rows, gated, tokens_moe, *weights)
+
+
+def token_kernel(chunks, block_ref, gain_ref, own_ref, in_ref, page_ref, all_ref, send_sem, recv_sem, local_sem):
+    tile = lax.axis_index("tile")
+    rows, width = block_ref.shape
+    tokens = own_ref.shape[0]
+    post = Sender(send_sem, recv_sem)
+    greet([{"tile": (tile + sign + NX) % NX} for sign in (1, -1)])
+
+    def at(block, part):
+        return all_ref.at[part, pl.ds(pl.multiple_of(block * width, width), width)]
+
+    arrivals = {}
+    for hop in (1, 2):
+        for sign, i in interleave(
+            [(1, i) for i in dir_order(chunks, 1)], [(-1, i) for i in dir_order(chunks, -1)]
+        ):
+            start, size, far = chunks[i]
+            if hop == 2 and far != sign:
+                continue
+            block, part = (tile - sign * (hop - 1) + NX) % NX, pl.ds(start, size)
+            if hop == 1:
+                source = block_ref.at[part]
+            else:
+                arrivals[(sign, i, 1)].wait_recv()
+                source = at(block, part)
+            arrivals[(sign, i, hop)] = post.send(
+                source, at(block, part), {"tile": (tile + sign + NX) % NX}
+            )
+        if hop == 1:
+            own = pltpu.make_async_copy(block_ref, at(tile, pl.ds(0, rows)), local_sem)
+            own.start()
+    for (sign, i, hop), copy in arrivals.items():
+        if hop == 2 or chunks[i][2] != sign:
+            copy.wait_recv()
+    own.wait()
+
+    def normed(values):
+        values = values.astype(jnp.float32)
+        mean = jnp.mean(values * values, axis=-1, keepdims=True)
+        return (values * lax.rsqrt(mean + norm_eps) * gain_ref[...]).astype(jnp.bfloat16)
+
+    for start in range(0, rows, tokens):
+        page_ref[start : start + tokens] = normed(all_ref[start : start + tokens])
+    mine = pl.ds(pl.multiple_of(tile * tokens, tokens), tokens)
+    own_ref[...] = all_ref[mine]
+    in_ref[...] = page_ref[mine]
+    for copy in post.made:
+        copy.wait_send()
+
+
+def gather_tokens(block, gain, tokens, collective_id):
+    rows, width = block.shape
+    chunks = ring_chunks(rows, tokens)
+    copies = copies_of("x", chunks)
+
+    def kernel(*refs):
+        token_kernel(chunks, *refs)
+
+    return pl.pallas_call(
+        kernel,
+        out_shape=[
+            jax.ShapeDtypeStruct((tokens, NX * width), block.dtype),
+            jax.ShapeDtypeStruct((tokens, NX * width), block.dtype),
+            jax.ShapeDtypeStruct((rows, NX * width), block.dtype),
+        ],
+        in_specs=[pl.BlockSpec(memory_space=pltpu.VMEM)] * 2,
+        out_specs=[pl.BlockSpec(memory_space=pltpu.VMEM)] * 3,
+        scratch_shapes=[
+            pltpu.VMEM((rows, NX * width), block.dtype),
+            pltpu.SemaphoreType.DMA((copies,)),
+            pltpu.SemaphoreType.DMA((copies,)),
+            pltpu.SemaphoreType.DMA,
         ],
         compiler_params=pltpu.CompilerParams(collective_id=collective_id, has_side_effects=True),
-    )(first, second, gated)
+    )(block, gain.reshape(1, -1))
 
 
 def slot_tables(table, tokens, top):
@@ -660,17 +786,20 @@
     side_a = [(t, t + 1 - 2 * (t % 2)) for t in range(NX)]
     side_b = [(t, NX - 1 - t) for t in range(NX)]
     units = expert_out.shape[1] // 2
-    gate_halves, up_halves = (
-        [expert_in[0, :, which, i * units : (i + 1) * units] for i in (0, 1)] for which in (0, 1)
-    )
-    out_halves = [expert_out[0, i * units : (i + 1) * units] for i in (0, 1)]
+    in_rows = expert_in[0].transpose(1, 2, 0)
+    gate_halves, up_halves, out_halves = (
+        [block[:units], block[units:]] for block in (in_rows[0], in_rows[1], expert_out[0])
+    )
 
     def swap(halves, after):
-        first, second, after = lax.optimization_barrier((halves[0], halves[1], after))
+        first, second = halves
+        if after is not None:
+            first, second, after = lax.optimization_barrier((first, second, after))
         from_a = lax.ppermute(first, "tile", side_a)
         from_b = lax.ppermute(second, "tile", side_b)
         return from_a, from_b, after
 
+    out_a, out_b, _ = swap(out_halves, None)
     project = lax.all_gather(proj_weight, "expert", axis=0, tiled=True)
 
     inputs = patches.reshape(local_rows, width_vit).astype(jnp.float32)
@@ -682,7 +811,7 @@
     table = table.at[:top, :tokens].set(own_routes.T.astype(jnp.float32))
     table = table.at[8 : 8 + top, :tokens].set(gates.reshape(tokens, top).T)
     piece, tables_z = ring_gather([("x", normed, 32), ("z", table, 16)], 0)
-    out_a, out_b, piece = swap(out_halves, piece)
+    gate_a, gate_b, piece = swap(gate_halves, piece)
     piece = piece.reshape(NX * local_rows, width_vit)
 
     heads_here = qkv_weight.shape[2] // HD
@@ -716,19 +845,13 @@
         .reshape(tokens, 4 * width_vit)
     )
     (group_merged,) = ring_gather([("x", merged, 16)], 2)
-    gate_a, gate_b, group_merged = swap(gate_halves, group_merged)
+    up_a, up_b, group_merged = swap(up_halves, group_merged)
     select, gated = slot_tables(tables_z, tokens, top)
     projected = jnp.dot(
         group_merged.reshape(NX * tokens, -1), project, preferred_element_type=jnp.float32
     ).astype(jnp.bfloat16)
-    (pieces,) = ring_gather([("x", projected, 32)], 3)
-    up_a, up_b, pieces = swap(up_halves, pieces)
-    page_tokens = pieces.transpose(1, 0, 2).reshape(NX * tokens, -1)
-    width_moe = page_tokens.shape[1]
-    page_in = rms_norm(page_tokens.astype(jnp.float32), moe_gain).astype(jnp.bfloat16)
-    tokens_moe = lax.dynamic_slice_in_dim(page_tokens, tile_id * tokens, tokens, 0)
-    moe_in = lax.dynamic_slice_in_dim(page_in, tile_id * tokens, tokens, 0)
-
+    tokens_moe, moe_in, page_in = gather_tokens(projected, moe_gain, tokens, 3)
+    width_moe = page_in.shape[1]
     shared_gated = jnp.dot(
         page_in, shared_in.reshape(width_moe, -1), preferred_element_type=jnp.float32
     ).reshape(NX * tokens, 2, -1)
@@ -739,32 +862,16 @@
         .reshape(NX, tokens, width_moe)
     )
 
-    arrived, shared_part = dispatch(moe_in, select, shared_rows, 4)
-    slots = GROUP * NZ * CAP
-    arrived = arrived.reshape(3 * slots, width_moe)
-
-    def feed_forward(rows, halves):
-        hidden_rows = []
-        for gate_piece, up_piece, _ in halves:
-            gate_rows = jnp.dot(rows, gate_piece, preferred_element_type=jnp.float32)
-            up_rows = jnp.dot(rows, up_piece, preferred_element_type=jnp.float32)
-            hidden_rows.append((jax.nn.silu(gate_rows) * up_rows).astype(jnp.bfloat16))
-        total = jnp.dot(
-            jnp.concatenate(hidden_rows, axis=1),
-            jnp.concatenate([out_piece for _, _, out_piece in halves]),
-            preferred_element_type=jnp.float32,
-        )
-        return total.astype(jnp.bfloat16).reshape(2, GROUP, NZ * CAP, width_moe)
-
-    second = feed_forward(
-        arrived[slots:], [(gate_halves[0], up_halves[0], out_halves[0]), (gate_a, up_a, out_a)]
-    )
-    first = feed_forward(
-        arrived[: 2 * slots], [(gate_halves[1], up_halves[1], out_halves[1]), (gate_b, up_b, out_b)]
-    )
-    routed = give_back(first, second, gated, tokens, 5)
-    output = tokens_moe.astype(jnp.float32) + shared_part + routed
-    return output.astype(jnp.bfloat16).reshape(1, row_count // 2, columns // 2, width_moe)
+    output = expert_layer(
+        moe_in,
+        select,
+        shared_rows,
+        gated,
+        tokens_moe,
+        (in_rows, expert_out[0], gate_a, up_a, out_a, gate_b, up_b, out_b),
+        4,
+    )
+    return output.reshape(1, row_count // 2, columns // 2, width_moe)
 
 
 def solution(mesh):

time: 299 us -> 274 us (0.916)
  matrix products: 42 us -> 20.5 us
  Pallas kernels: 197 us -> 209 us
  other arithmetic: 17.3 us -> 10.6 us
  local copies, waits for them, and re-layouts: 15.9 us -> 11.7 us
  waiting for transfers between devices: 3.99 us -> 0.73 us
    pallas_call x2, Pallas kernels: 123 us -> 159 us  [the longest x1 121 us: expert_layer(): pl.pallas_call(expert_kernel, out_shape=jax.ShapeDtypeStruct((tokens, wid...]
    pallas_call x3 -> x2, Pallas kernels: 61.3 us -> 38.1 us  [ring_gather(): pl.pallas_call(kernel, out_shape=[jax.ShapeDtypeStruct((sizes[axis],) + b...]
    dot_general x10 -> x0, matrix products: 21.5 us -> none  [the longest x2 9.63 us: feed_forward(): jnp.dot(jnp.concatenate(hidden_rows, axis=1), jnp.concatenate([out_piece...]
    squeeze x2 -> x0, local copies, waits for them, and re-layouts: 6.1 us -> none  [the longest x1 3.5 us: per_device(): expert_in[0, :, which, i * units:(i + 1) * units]]
    convert_element_type x3 -> x1, other arithmetic: 4.48 us -> 0.01 us  [slot_tables(): ranked = rank[:, None, :] == (slot % CAP).astype(jnp.float32)[None, :, None]]
    ppermute x3, waiting for transfers between devices: 3.27 us -> 0.01 us  [swap(): from_a = lax.ppermute(first, 'tile', side_a)]
    slice x1 -> x2, local copies, waits for them, and re-layouts: 3.57 us -> 6.18 us  [per_device(): block[units:]]
  transfers between devices with their start and end apart: 7 -> 7, of which waited for: 1 -> 0; matrix products, arithmetic and copies ran while one was open for 23% -> 15% of each run, Pallas kernels for 46% -> 32%
where the time goes in v1:
time: 274 us; the launch traced here: 273 us
  Pallas kernels  209 us (76%)
  matrix products  20.5 us (7%)
  between operations  13.7 us (5%)
  local copies, waits for them, and re-layouts  11.7 us (4%)
  other arithmetic  10.6 us (4%)
  starting transfers between devices  7.47 us (3%)
    pallas_call x1, Pallas kernels, expert_layer(): pl.pallas_call(expert_kernel, out_shape=jax.ShapeDtypeStruct((tokens, wid...  121 us
    pallas_call x2, Pallas kernels, ring_gather(): pl.pallas_call(kernel, out_shape=[jax.ShapeDtypeStruct((sizes[axis],) + b...  38.1 us
    pallas_call x1, Pallas kernels, gather_tokens(): pl.pallas_call(kernel, out_shape=[jax.ShapeDtypeStruct((tokens, NX * widt...  37.8 us
    pallas_call x1, Pallas kernels, ring_reduce(): pl.pallas_call(kernel, out_shape=[jax.ShapeDtypeStruct(block.shape[1:], k...  11.9 us
    slice x2, local copies, waits for them, and re-layouts, per_device(): block[units:]  6.18 us
  transfers between devices with their start and end apart: 7, of which 0 were waited for; matrix products, arithmetic and copies ran while one was open for 15% of the time, Pallas kernels for 32%

profile of v1, /device:TPU:8, one launch (start us, length us, event | category | flops | bytes accessed | tf_op | source)
XLA Modules:
  0.0 273.3 jit_solution(17583725553845035281)
XLA Ops:
  6.5 0.0 copy-start
  6.5 0.7 all-gather.2.cloned.1.call-update
  7.3 1.2 convert_reduce_fusion
  8.5 0.1 div.89
  8.6 1.2 fusion.10
  9.8 0.1 rsqrt.20
  9.9 0.8 reshape.409
  10.7 0.8 reshape.410
  11.5 0.4 scatter.9.refs_1_
  11.9 0.0 copy-start.7
  11.9 1.9 fusion.13.refs_0_
  13.8 23.8 %shard_map.145 = (bf16[4,128,1152]{2,1,0:T(8,128)(2,1)}, f32[8,16,128]{2,1,0:T(8,128)}) custom-call(bf16[128,1152]{1,0:T(8,128)(2,1)} %fusion.13.refs_0_, f32[16,128]{1,0:T(8,128)} %copy-done.7), custom_call_target="tpu_custom_call" | custom-call | tf_op jit(solution)/shard_map/pallas_call | solution.py:172
  37.6 0.0 copy-start.9
  37.6 3.5 %slice_bitcast_fusion = (bf16[176,2048]{1,0:T(8,128)(2,1)}, bf16[176,2048]{1,0:T(8,128)(2,1)}, bf16[176,2048]{1,0:T(8,128)(2,1)}, bf16[176,2048]{1,0:T(8,128)(2,1)}) fusion(bf16[2,352,2048]{2,1,0:T(8,128)(2,1)} %bitcast.130), kind=kLoop, calls=%fused_computation.14 | loop fusion | bytes 5767168 | tf_op jit(solution)/shard_map/slice | solution.py:791
  41.1 0.9 collective-permute-start
  42.0 0.1 add.156
  42.1 0.4 multiply_cosine_fusion.1
  42.5 3.3 %convolution_add_fusion = f32[512,3,4,72]{0,3,2,1:T(8,128)S(1)} fusion(bf16[512,1152,1,1]{1,0,3,2:T(8,128)(2,1)} %bitcast.141, bf16[3,4,72,1152]{3,2,1,0:T(8,128)(2,1)} %bitcast.140, f32[3,4,72]{2,1,0:T(4,128)S(1)} %add.156), kind=kOutput, calls=%fused_computation.11 | convolution fusion | flops 1019658240 | bytes 4943232 | tf_op jit(solution)/shard_map/dot_general | solution.py:820
  45.8 0.1 slice_bitcast_fusion.7
  45.9 0.1 subtract_convert_fusion.1
  46.1 1.0 subtract_convert_fusion.3
  47.1 0.0 copy-done.4
  47.1 4.6 %fusion.57 = (f32[4,512]{1,0:T(4,128)S(1)}, f32[4,512,512]{1,2,0:T(8,128)}) fusion(bf16[512,4,18]{0,2,1:T(8,128)(2,1)S(1)} %get-tuple-element.69, bf16[512,4,18]{0,2,1:T(8,128)(2,1)S(1)} %get-tuple-element.70, bf16[512,4,18]{0,2,1:T(8,128)(2,1)S(1)} %get-tuple-element.64, bf16[512,4,18]{0,2,1:T(8,128)(2,1)S(1)} %get-tuple-element.63, ...), kind=kOutput, calls=%fused_computation.121 | convolution fusion | flops 156500480 | bytes 4792320 | tf_op jit(solution)/shard_map/sub | solution.py:58
  51.7 2.9 %fusion.8 = bf16[4,72,512]{2,1,0:T(8,128)(2,1)S(1)} fusion(f32[4,512,512]{1,2,0:T(8,128)} %get-tuple-element.80, f32[4,512]{1,0:T(4,128)S(1)} %get-tuple-element.79, f32[512,3,4,72]{0,3,2,1:T(8,128)} %copy-done.4), kind=kOutput, calls=%fused_computation.12 | convolution fusion | flops 153239552 | bytes 4792320 | tf_op jit(solution)/shard_map/hqk,khd->qhd/dot_general | solution.py:59
  54.6 0.0 copy-start.1
  54.6 0.0 copy-start.5
  54.6 2.0 convolution_convert_fusion
  56.6 11.9 %shard_map.146 = f32[128,1152]{1,0:T(8,128)} custom-call(bf16[4,128,1152]{2,1,0:T(8,128)(2,1)} %bitcast.135), custom_call_target="tpu_custom_call" | custom-call | tf_op jit(solution)/shard_map/pallas_call | solution.py:268
  68.6 1.3 fusion.28
  69.9 1.3 multiply_reduce_fusion.1
  71.2 0.0 copy-done.2
  71.2 0.2 multiply_convert_fusion
  71.3 0.1 reshape.415
  71.5 0.2 copy.35
  71.7 0.9 reshape.416.refs_0_
  72.6 14.3 %shard_map.147 = bf16[4,32,4608]{2,1,0:T(8,128)(2,1)} custom-call(bf16[32,4608]{1,0:T(8,128)(2,1)} %reshape.416.refs_0_), custom_call_target="tpu_custom_call" | custom-call | tf_op jit(solution)/shard_map/pallas_call | solution.py:172
  86.9 1.0 collective-permute-start.1
  87.9 2.7 slice_bitcast_fusion.4
  90.7 1.1 collective-permute-start.2
  91.8 1.2 collective-permute-start.3
  93.0 2.0 collective-permute-start.4
  95.1 0.1 eq.87
  95.2 0.1 eq.77
  95.3 0.1 broadcast_in_dim.20
  95.3 0.1 compare_reduce_fusion
  95.4 0.2 fusion.24
  95.6 0.1 broadcast_compare_fusion
  95.7 0.8 fusion.20.select_ref
  96.5 0.1 fusion.33
  96.6 0.9 bitcast_select_fusion.gated_ref
  97.5 0.0 collective-permute-done.gate_a_ref
  97.5 1.2 collective-permute-start.5
  98.7 4.1 %convolution_convert_fusion.2.refs_0_ = bf16[128,512]{1,0:T(8,128)(2,1)} fusion(bf16[128,4608]{1,0:T(8,128)(2,1)} %bitcast.133, bf16[4608,512]{1,0:T(8,128)(2,1)} %all-gather.2.cloned.1.call-done), kind=kOutput, calls=%fused_computation.13 | convolution fusion | flops 604045312 | bytes 6029312 | tf_op jit(solution)/shard_map/dot_general | solution.py:850
  102.9 37.8 %shard_map.148 = (bf16[32,2048]{1,0:T(8,128)(2,1)}, bf16[32,2048]{1,0:T(8,128)(2,1)}, bf16[128,2048]{1,0:T(8,128)(2,1)}) custom-call(bf16[128,512]{1,0:T(8,128)(2,1)} %convolution_convert_fusion.2.refs_0_, f32[1,2048]{1,0:T(1,128)} %bitcast.139), custom_call_target="tpu_custom_call" | custom-call | tf_op jit(solution)/shard_map/pallas_call | solution.py:719
  140.7 0.0 copy-start.3
  140.7 2.1 fusion.4
  142.8 1.3 convolution_convert_fusion.1
  144.1 0.0 collective-permute-done.1.up_a_ref
  144.1 0.0 collective-permute-done.2.down_a_ref
  144.1 0.0 collective-permute-done.3.gate_b_ref
  144.1 0.0 collective-permute-done.4.up_b_ref
  144.1 0.0 collective-permute-done.5.down_b_ref
  144.1 120.8 %shard_map.149 = bf16[32,2048]{1,0:T(8,128)(2,1)} custom-call(bf16[32,2048]{1,0:T(8,128)(2,1)} %get-tuple-element.43.rows_ref, bf16[384,256]{1,0:T(8,128)(2,1)} %fusion.20.select_ref, bf16[4,32,2048]{2,1,0:T(8,128)(2,1)} %bitcast.134, f32[384,256]{1,0:T(8,128)} %bitcast_select_fusion.gated_ref, bf16[32,2048]{1,0:T(8,128)(2,1)} %get-tuple-element.46.tokens_ref, ...), custom_call_target="tpu_custom_call" | custom-call | tf_op jit(solution)/shard_map/pallas_call | solution.py:625
  264.9 1.6 copy.38
  (33 shorter events, 0.1 us)
Async XLA Ops:
  6.5 134.2 %copy-start = (bf16[2048,2,352]{0,2,1:T(8,128)(2,1)S(1)}, bf16[2048,2,352]{0,2,1:T(8,128)(2,1)}, u32[]{:S(2)}) copy-start(bf16[2048,2,352]{0,2,1:T(8,128)(2,1)} %param.30) | copy-start | bytes 8650756
  6.5 92.2 %all-gather.2.cloned.1.call-start = ((), (), s32[]{:S(2)}) async-start(), calls=%async_computation | async-start | bytes 4792320 | tf_op jit(solution)/shard_map/all_gather | solution.py:803
  11.9 1.9 copy-start.7
  37.6 4.4 %copy-start.9 = (f32[3,288]{1,0:T(4,128)S(1)}, f32[3,288]{1,0:T(4,128)}, u32[]{:S(2)}) copy-start(f32[3,288]{1,0:T(4,128)} %param.22) | copy-start | bytes 10372
  41.1 56.4 %collective-permute-start = (bf16[176,2048]{1,0:T(8,128)(2,1)}, bf16[176,2048]{1,0:T(8,128)(2,1)}, u32[]{:S(2)}, u32[]{:S(2)}) collective-permute-start(bf16[176,2048]{1,0:T(8,128)(2,1)} %get-tuple-element.47), channel_id=1, source_target_pairs={{0,64},{64,0},{128,192},{192,128},{1,65},{65,1},{129,193},{193,129... | collective-permute-start | bytes 2162696 | tf_op jit(solution)/shard_map/ppermute | solution.py:798
  45.8 1.3 copy-start.4
  51.7 2.9 %copy-start.10 = (bf16[288,1152]{1,0:T(8,128)(2,1)S(1)}, bf16[288,1152]{1,0:T(8,128)(2,1)}, u32[]{:S(2)}) copy-start(bf16[288,1152]{1,0:T(8,128)(2,1)} %param.23) | copy-start | bytes 1990660
  54.6 13.9 %copy-start.1 = (bf16[1,4,32,1152]{3,2,1,0:T(8,128)(2,1)S(1)}, bf16[1,4,32,1152]{3,2,1,0:T(8,128)(2,1)}, u32[]{:S(2)}) copy-start(bf16[1,4,32,1152]{3,2,1,0:T(8,128)(2,1)} %param.19) | copy-start | bytes 884740
  54.6 13.9 %copy-start.5 = (f32[1152]{0:T(1024)S(1)}, f32[1152]{0:T(1024)}, u32[]{:S(2)}) copy-start(f32[1152]{0:T(1024)} %param.24) | copy-start | bytes 13828
  56.6 14.6 %copy-start.8 = (f32[1152]{0:T(1024)S(1)}, f32[1152]{0:T(1024)}, u32[]{:S(2)}) copy-start(f32[1152]{0:T(1024)} %param.25) | copy-start | bytes 13828
  68.6 2.6 copy-start.2
  72.6 22.4 %copy-start.6 = (f32[8,16,128]{2,1,0:T(8,128)S(1)}, f32[8,16,128]{2,1,0:T(8,128)}, u32[]{:S(2)}) copy-start(f32[8,16,128]{2,1,0:T(8,128)} %get-tuple-element.44) | copy-start | bytes 196612
  86.9 57.1 %collective-permute-start.1 = (bf16[176,2048]{1,0:T(8,128)(2,1)}, bf16[176,2048]{1,0:T(8,128)(2,1)}, u32[]{:S(2)}, u32[]{:S(2)}) collective-permute-start(bf16[176,2048]{1,0:T(8,128)(2,1)} %get-tuple-element.48), channel_id=1, source_target_pairs={{0,64},{64,0},{128,192},{192,128},{1,65},{65,1},{129,193},{193,129... | collective-permute-start | bytes 2162696 | tf_op jit(solution)/shard_map/ppermute | solution.py:798
  90.7 53.4 %collective-permute-start.2 = (bf16[176,2048]{1,0:T(8,128)(2,1)}, bf16[176,2048]{1,0:T(8,128)(2,1)}, u32[]{:S(2)}, u32[]{:S(2)}) collective-permute-start(bf16[176,2048]{1,0:T(8,128)(2,1)} %get-tuple-element.58), channel_id=1, source_target_pairs={{0,64},{64,0},{128,192},{192,128},{1,65},{65,1},{129,193},{193,129... | collective-permute-start | bytes 2162696 | tf_op jit(solution)/shard_map/ppermute | solution.py:798
  91.8 52.3 %collective-permute-start.3 = (bf16[176,2048]{1,0:T(8,128)(2,1)}, bf16[176,2048]{1,0:T(8,128)(2,1)}, u32[]{:S(2)}, u32[]{:S(2)}) collective-permute-start(bf16[176,2048]{1,0:T(8,128)(2,1)} %get-tuple-element.49), channel_id=1, source_target_pairs={{0,192},{64,128},{128,64},{192,0},{1,193},{65,129},{129,65},{193,1... | collective-permute-start | bytes 2162696 | tf_op jit(solution)/shard_map/ppermute | solution.py:799
  93.0 51.1 %collective-permute-start.4 = (bf16[176,2048]{1,0:T(8,128)(2,1)}, bf16[176,2048]{1,0:T(8,128)(2,1)}, u32[]{:S(2)}, u32[]{:S(2)}) collective-permute-start(bf16[176,2048]{1,0:T(8,128)(2,1)} %get-tuple-element.50), channel_id=1, source_target_pairs={{0,192},{64,128},{128,64},{192,0},{1,193},{65,129},{129,65},{193,1... | collective-permute-start | bytes 2162696 | tf_op jit(solution)/shard_map/ppermute | solution.py:799
  97.5 46.6 %collective-permute-start.5 = (bf16[176,2048]{1,0:T(8,128)(2,1)}, bf16[176,2048]{1,0:T(8,128)(2,1)}, u32[]{:S(2)}, u32[]{:S(2)}) collective-permute-start(bf16[176,2048]{1,0:T(8,128)(2,1)} %get-tuple-element.57), channel_id=1, source_target_pairs={{0,192},{64,128},{128,64},{192,0},{1,193},{65,129},{129,65},{193,1... | collective-permute-start | bytes 2162696 | tf_op jit(solution)/shard_map/ppermute | solution.py:799
  140.7 2.1 copy-start.3
Sparse Core Ops, SparseCore 0:
  10.1 80.6 all-gather.1

commit v2 on v1

--- a/solution.py
+++ b/solution.py
@@ -277,7 +277,7 @@
     )(*[block for _, block, _, _ in tasks])
 
 
-CHUNKS = 4
+CHUNKS = 2
 
 
 def places():
@@ -330,7 +330,7 @@
 
 def expert_kernel(
     rows_ref, select_ref, shared_ref, gated_ref, tokens_ref, in_ref, down_ref,
-    gate_a_ref, up_a_ref, down_a_ref, gate_b_ref, up_b_ref, down_b_ref,
+    gate_a_ref, gate_b_ref,
     out_ref,
     ring_ref, chosen_ref, sum_land_ref, sum_stage_ref, slots_ref, weight_ref, hidden_ref, part_ref,
     high_ref, low_ref, side_ref, stage_ref, back_ref, mix_ref, land_ref, step_ref, base_ref,
@@ -340,7 +340,7 @@
     tokens, width = rows_ref.shape
     chunk, half_rows = width // CHUNKS, tokens // 2
     slots = NZ * CAP
-    units = down_a_ref.shape[0]
+    units = gate_a_ref.shape[0]
     post = Sender(send_sem, recv_sem)
     peers = [(me + k) % GROUP for k in range(1, GROUP)]
     low_units, high_units = pl.ds(0, units), pl.ds(units, units)
@@ -350,14 +350,10 @@
         ((0, 0, 1), in_ref.at[1, high_units]),
         ((0, 0, 2), down_ref.at[high_units]),
         ((0, 1, 0), gate_b_ref),
-        ((0, 1, 1), up_b_ref),
-        ((0, 1, 2), down_b_ref),
         ((1, 0, 0), in_ref.at[0, low_units]),
         ((1, 0, 1), in_ref.at[1, low_units]),
         ((1, 0, 2), down_ref.at[low_units]),
         ((1, 1, 0), gate_a_ref),
-        ((1, 1, 1), up_a_ref),
-        ((1, 1, 2), down_a_ref),
     ):
         copy = pltpu.make_async_copy(source, weight_ref.at[where], weight_sem.at[len(loads)])
         copy.start()
@@ -410,6 +406,11 @@
             sums[(sign, half, step)] = (copy, slot)
 
     shared_step(0)
+    swapped = [
+        post.send(source.at[half_units], weight_ref.at[1 - side, 1, kind], across[side])
+        for kind, source in ((1, in_ref.at[1]), (2, down_ref))
+        for side, half_units in ((0, low_units), (1, high_units))
+    ]
     for j in range(CHUNKS):
         ring_ref[j, z] = rows_ref[:, j * chunk : (j + 1) * chunk]
     gated = gated_ref[...].T
@@ -458,9 +459,7 @@
         j = wave - (Z_HALF - 1)
         if 0 <= j < CHUNKS:
             choose(j)
-        if 0 <= j - 2 < CHUNKS:
-            forward(j - 2)
-    for j in range(CHUNKS - 2, CHUNKS):
+    for j in range(CHUNKS):
         forward(j)
 
     def feed_forward(which, mine, job):
@@ -503,6 +502,8 @@
 
     for copy in loads + own:
         copy.wait()
+    for copy in swapped:
+        copy.wait_recv()
 
     def own_job(i, carry):
         feed_forward(i % 2, 1, i // 2)
@@ -617,7 +618,7 @@
     chunk = width // CHUNKS
     kind = rows.dtype
     units = weights[-1].shape[0]
-    copies = CHUNKS * (2 * Z_COPIES + 2 * (GROUP - 1) + 2 * GROUP) + X_COPIES
+    copies = CHUNKS * (2 * Z_COPIES + 2 * (GROUP - 1) + 2 * GROUP) + X_COPIES + 4
     boxes = pltpu.VMEM((CHUNKS, len(Z_STREAMS) * Z_HALF, tokens // 2, chunk), kind)
     blocks = pltpu.VMEM((CHUNKS, GROUP, slots, chunk), kind)
     shared_boxes = pltpu.VMEM((X_COPIES, tokens // 2, width), kind)
@@ -649,7 +650,7 @@
             pltpu.SemaphoreType.DMA((copies,)),
             pltpu.SemaphoreType.DMA((copies,)),
             pltpu.SemaphoreType.DMA((CHUNKS,)),
-            pltpu.SemaphoreType.DMA((12,)),
+            pltpu.SemaphoreType.DMA((8,)),
             pltpu.SemaphoreType.DMA((2 * CHUNKS * GROUP,)),
             pltpu.SemaphoreType.DMA((2 * CHUNKS * GROUP,)),
         ],
@@ -787,19 +788,14 @@
     side_b = [(t, NX - 1 - t) for t in range(NX)]
     units = expert_out.shape[1] // 2
     in_rows = expert_in[0].transpose(1, 2, 0)
-    gate_halves, up_halves, out_halves = (
-        [block[:units], block[units:]] for block in (in_rows[0], in_rows[1], expert_out[0])
-    )
+    gate_halves = in_rows[0, :units], in_rows[0, units:]
 
     def swap(halves, after):
-        first, second = halves
-        if after is not None:
-            first, second, after = lax.optimization_barrier((first, second, after))
+        first, second, after = lax.optimization_barrier((*halves, after))
         from_a = lax.ppermute(first, "tile", side_a)
         from_b = lax.ppermute(second, "tile", side_b)
         return from_a, from_b, after
 
-    out_a, out_b, _ = swap(out_halves, None)
     project = lax.all_gather(proj_weight, "expert", axis=0, tiled=True)
 
     inputs = patches.reshape(local_rows, width_vit).astype(jnp.float32)
@@ -845,7 +841,6 @@
         .reshape(tokens, 4 * width_vit)
     )
     (group_merged,) = ring_gather([("x", merged, 16)], 2)
-    up_a, up_b, group_merged = swap(up_halves, group_merged)
     select, gated = slot_tables(tables_z, tokens, top)
     projected = jnp.dot(
         group_merged.reshape(NX * tokens, -1), project, preferred_element_type=jnp.float32
@@ -868,7 +863,7 @@
         shared_rows,
         gated,
         tokens_moe,
-        (in_rows, expert_out[0], gate_a, up_a, out_a, gate_b, up_b, out_b),
+        (in_rows, expert_out[0], gate_a, gate_b),
         4,
     )
     return output.reshape(1, row_count // 2, columns // 2, width_moe)

time: 274 us -> 256 us (0.934)
  Pallas kernels: 209 us -> 195 us
  starting transfers between devices: 7.47 us -> 2.18 us
  local copies, waits for them, and re-layouts: 11.7 us -> 8.25 us
    pallas_call x1, Pallas kernels: 37.8 us -> 12.3 us  [gather_tokens(): pl.pallas_call(kernel, out_shape=[jax.ShapeDtypeStruct((tokens, NX * widt...]
    pallas_call x1, Pallas kernels: 121 us -> 134 us  [expert_layer(): pl.pallas_call(expert_kernel, out_shape=jax.ShapeDtypeStruct((tokens, wid...]
    slice x2 -> x0, local copies, waits for them, and re-layouts: 6.18 us -> none  [per_device(): block[units:]]
    ppermute x3 -> x1, starting transfers between devices: 4.45 us -> 1.25 us  [swap(): from_b = lax.ppermute(second, 'tile', side_b)]
  transfers between devices with their start and end apart: 7 -> 3, of which waited for: 0 -> 1; matrix products, arithmetic and copies ran while one was open for 15% -> 15% of each run, Pallas kernels for 32% -> 24%
where the time goes in v2:
time: 256 us; the launch traced here: 253 us
  Pallas kernels  195 us (76%)
  matrix products  20.4 us (8%)
  between operations  13.7 us (5%)
  other arithmetic  10.5 us (4%)
  local copies, waits for them, and re-layouts  8.25 us (3%)
  waiting for transfers between devices  3.33 us (1%)
    pallas_call x1, Pallas kernels, expert_layer(): pl.pallas_call(expert_kernel, out_shape=jax.ShapeDtypeStruct((tokens, wid...  134 us
    pallas_call x2, Pallas kernels, ring_gather(): pl.pallas_call(kernel, out_shape=[jax.ShapeDtypeStruct((sizes[axis],) + b...  36.1 us
    pallas_call x1, Pallas kernels, ring_reduce(): pl.pallas_call(kernel, out_shape=[jax.ShapeDtypeStruct(block.shape[1:], k...  12.4 us
    pallas_call x1, Pallas kernels, gather_tokens(): pl.pallas_call(kernel, out_shape=[jax.ShapeDtypeStruct((tokens, NX * widt...  12.3 us
  transfers between devices with their start and end apart: 3, of which 1 were waited for; matrix products, arithmetic and copies ran while one was open for 15% of the time, Pallas kernels for 24%

profile of v2, /device:TPU:8, one launch (start us, length us, event | category | flops | bytes accessed | tf_op | source)
XLA Modules:
  0.0 253.2 jit_solution(11157084458115999713)
XLA Ops:
  6.5 0.0 copy-start
  6.5 0.0 all-gather.2.cloned.1.call-start
  6.5 0.7 all-gather.2.cloned.1.call-update
  7.3 1.0 reshape.403
  8.2 0.8 reshape.404
  9.0 1.1 convert_reduce_fusion
  10.1 0.1 div.89
  10.2 1.2 fusion.10
  11.3 0.0 copy-start.9
  11.4 0.1 rsqrt.20
  11.5 0.4 scatter.9.refs_1_
  11.9 0.0 copy-start.7
  11.9 1.9 fusion.13.refs_0_
  13.8 0.0 copy-done.7
  13.8 23.7 %shard_map.145 = (bf16[4,128,1152]{2,1,0:T(8,128)(2,1)}, f32[8,16,128]{2,1,0:T(8,128)}) custom-call(bf16[128,1152]{1,0:T(8,128)(2,1)} %fusion.13.refs_0_, f32[16,128]{1,0:T(8,128)} %copy-done.7), custom_call_target="tpu_custom_call" | custom-call | tf_op jit(solution)/shard_map/pallas_call | solution.py:172
  37.6 2.7 %slice_bitcast_fusion = (bf16[176,2048]{1,0:T(8,128)(2,1)}, bf16[176,2048]{1,0:T(8,128)(2,1)}) fusion(bf16[2,352,2048]{2,1,0:T(8,128)(2,1)} %bitcast.122), kind=kLoop, calls=%fused_computation.14 | loop fusion | bytes 2883584 | tf_op jit(solution)/shard_map/squeeze | solution.py:791
  40.2 0.9 collective-permute-start
  41.2 1.3 collective-permute-start.1
  42.4 0.0 copy-done.9
  42.4 0.1 add.156
  42.5 0.4 multiply_cosine_fusion.1
  42.9 3.3 %convolution_add_fusion = f32[512,3,4,72]{0,3,2,1:T(8,128)S(1)} fusion(bf16[512,1152,1,1]{1,0,3,2:T(8,128)(2,1)} %bitcast.133, bf16[3,4,72,1152]{3,2,1,0:T(8,128)(2,1)} %bitcast.132, f32[3,4,72]{2,1,0:T(4,128)S(1)} %add.156), kind=kOutput, calls=%fused_computation.11 | convolution fusion | flops 1019658240 | bytes 4943232 | tf_op jit(solution)/shard_map/dot_general | solution.py:816
  46.2 0.0 copy-start.4
  46.2 0.1 slice_bitcast_fusion.3
  46.3 0.1 subtract_convert_fusion.3
  46.5 1.0 subtract_convert_fusion.1
  47.5 0.0 copy-done.4
  47.5 4.5 %fusion.57 = (f32[4,512]{1,0:T(4,128)S(1)}, f32[4,512,512]{1,2,0:T(8,128)}) fusion(bf16[512,4,18]{0,2,1:T(8,128)(2,1)} %get-tuple-element.59, bf16[512,4,18]{0,2,1:T(8,128)(2,1)} %get-tuple-element.60, bf16[512,4,18]{0,2,1:T(8,128)(2,1)S(1)} %get-tuple-element.54, bf16[512,4,18]{0,2,1:T(8,128)(2,1)S(1)} %get-tuple-element.53, ...), kind=kOutput, calls=%fused_computation.117 | convolution fusion | flops 156500480 | bytes 4792320 | tf_op jit(solution)/shard_map/sub | solution.py:58
  52.0 2.9 %fusion.8 = bf16[4,72,512]{2,1,0:T(8,128)(2,1)S(1)} fusion(f32[4,512,512]{1,2,0:T(8,128)} %get-tuple-element.70, f32[4,512]{1,0:T(4,128)S(1)} %get-tuple-element.69, f32[512,3,4,72]{0,3,2,1:T(8,128)} %copy-done.4), kind=kOutput, calls=%fused_computation.12 | convolution fusion | flops 153239552 | bytes 4792320 | tf_op jit(solution)/shard_map/hqk,khd->qhd/dot_general | solution.py:59
  54.9 0.0 copy-done.10
  54.9 0.0 copy-start.1
  54.9 0.0 copy-start.5
  54.9 1.9 convolution_convert_fusion
  56.9 12.4 %shard_map.146 = f32[128,1152]{1,0:T(8,128)} custom-call(bf16[4,128,1152]{2,1,0:T(8,128)(2,1)} %bitcast.127), custom_call_target="tpu_custom_call" | custom-call | tf_op jit(solution)/shard_map/pallas_call | solution.py:268
  69.2 0.0 copy-done.1
  69.2 0.0 copy-done.5
  69.3 0.0 copy-start.2
  69.3 1.3 fusion.28
  70.6 1.3 multiply_reduce_fusion.1
  71.9 0.2 multiply_convert_fusion
  72.0 0.1 reshape.409
  72.2 0.2 copy.35
  72.4 0.9 reshape.410.refs_0_
  73.3 12.4 %shard_map.147 = bf16[4,32,4608]{2,1,0:T(8,128)(2,1)} custom-call(bf16[32,4608]{1,0:T(8,128)(2,1)} %reshape.410.refs_0_), custom_call_target="tpu_custom_call" | custom-call | tf_op jit(solution)/shard_map/pallas_call | solution.py:172
  85.7 0.1 eq.77
  85.8 0.1 broadcast_in_dim.20
  85.9 0.1 eq.87
  86.0 0.1 compare_reduce_fusion
  86.1 0.2 fusion.24
  86.3 0.1 broadcast_compare_fusion
  86.4 0.8 fusion.20.select_ref
  87.2 0.1 fusion.33
  87.3 0.9 bitcast_select_fusion.gated_ref
  88.2 2.6 %all-gather.2.cloned.1.call-done = bf16[4608,512]{1,0:T(8,128)(2,1)} async-done(((bf16[72,512]{1,0:T(8,128)(2,1)}), bf16[4608,512]{1,0:T(8,128)(2,1)}) %all-gather.2.cloned.1.call-update) | async-done | bytes 4718608 | tf_op jit(solution)/shard_map/all_gather | solution.py:799
  90.8 4.1 %convolution_convert_fusion.2.refs_0_ = bf16[128,512]{1,0:T(8,128)(2,1)} fusion(bf16[128,4608]{1,0:T(8,128)(2,1)} %bitcast.124, bf16[4608,512]{1,0:T(8,128)(2,1)} %all-gather.2.cloned.1.call-done), kind=kOutput, calls=%fused_computation.13 | convolution fusion | flops 604045312 | bytes 6029312 | tf_op jit(solution)/shard_map/dot_general | solution.py:845
  94.9 12.3 %shard_map.148 = (bf16[32,2048]{1,0:T(8,128)(2,1)}, bf16[32,2048]{1,0:T(8,128)(2,1)}, bf16[128,2048]{1,0:T(8,128)(2,1)}) custom-call(bf16[128,512]{1,0:T(8,128)(2,1)} %convolution_convert_fusion.2.refs_0_, f32[1,2048]{1,0:T(1,128)} %bitcast.131), custom_call_target="tpu_custom_call" | custom-call | tf_op jit(solution)/shard_map/pallas_call | solution.py:720
  107.3 0.0 copy-start.3
  107.3 0.0 copy-done
  107.3 2.1 fusion.4
  109.4 1.3 convolution_convert_fusion.1
  110.7 0.0 collective-permute-done.gate_a_ref
  110.7 0.0 collective-permute-done.1.gate_b_ref
  110.7 134.1 %shard_map.149 = bf16[32,2048]{1,0:T(8,128)(2,1)} custom-call(bf16[32,2048]{1,0:T(8,128)(2,1)} %get-tuple-element.39.rows_ref, bf16[384,256]{1,0:T(8,128)(2,1)} %fusion.20.select_ref, bf16[4,32,2048]{2,1,0:T(8,128)(2,1)} %bitcast.125, f32[384,256]{1,0:T(8,128)} %bitcast_select_fusion.gated_ref, bf16[32,2048]{1,0:T(8,128)(2,1)} %get-tuple-element.42.tokens_ref, ...), custom_call_target="tpu_custom_call" | custom-call | tf_op jit(solution)/shard_map/pallas_call | solution.py:626
  244.8 1.6 copy.38
  (24 shorter events, 0.1 us)
Async XLA Ops:
  6.5 100.7 %copy-start = (bf16[2048,2,352]{0,2,1:T(8,128)(2,1)S(1)}, bf16[2048,2,352]{0,2,1:T(8,128)(2,1)}, u32[]{:S(2)}) copy-start(bf16[2048,2,352]{0,2,1:T(8,128)(2,1)} %param.30) | copy-start | bytes 8650756
  6.5 84.3 %all-gather.2.cloned.1.call-start = ((), (), s32[]{:S(2)}) async-start(), calls=%async_computation | async-start | bytes 4792320 | tf_op jit(solution)/shard_map/all_gather | solution.py:799
  11.3 31.1 %copy-start.9 = (f32[3,288]{1,0:T(4,128)S(1)}, f32[3,288]{1,0:T(4,128)}, u32[]{:S(2)}) copy-start(f32[3,288]{1,0:T(4,128)} %param.22) | copy-start | bytes 10372
  11.9 1.9 copy-start.7
  40.2 70.4 %collective-permute-start = (bf16[176,2048]{1,0:T(8,128)(2,1)}, bf16[176,2048]{1,0:T(8,128)(2,1)}, u32[]{:S(2)}, u32[]{:S(2)}) collective-permute-start(bf16[176,2048]{1,0:T(8,128)(2,1)} %get-tuple-element.43), channel_id=1, source_target_pairs={{0,64},{64,0},{128,192},{192,128},{1,65},{65,1},{129,193},{193,129... | collective-permute-start | bytes 2162696 | tf_op jit(solution)/shard_map/ppermute | solution.py:795
  41.2 69.5 %collective-permute-start.1 = (bf16[176,2048]{1,0:T(8,128)(2,1)}, bf16[176,2048]{1,0:T(8,128)(2,1)}, u32[]{:S(2)}, u32[]{:S(2)}) collective-permute-start(bf16[176,2048]{1,0:T(8,128)(2,1)} %get-tuple-element.44), channel_id=1, source_target_pairs={{0,192},{64,128},{128,64},{192,0},{1,193},{65,129},{129,65},{193,1... | collective-permute-start | bytes 2162696 | tf_op jit(solution)/shard_map/ppermute | solution.py:796
  46.2 1.3 copy-start.4
  52.0 2.9 %copy-start.10 = (bf16[288,1152]{1,0:T(8,128)(2,1)S(1)}, bf16[288,1152]{1,0:T(8,128)(2,1)}, u32[]{:S(2)}) copy-start(bf16[288,1152]{1,0:T(8,128)(2,1)} %param.23) | copy-start | bytes 1990660
  54.9 14.3 %copy-start.1 = (bf16[1,4,32,1152]{3,2,1,0:T(8,128)(2,1)S(1)}, bf16[1,4,32,1152]{3,2,1,0:T(8,128)(2,1)}, u32[]{:S(2)}) copy-start(bf16[1,4,32,1152]{3,2,1,0:T(8,128)(2,1)} %param.19) | copy-start | bytes 884740
  54.9 14.3 %copy-start.5 = (f32[1152]{0:T(1024)S(1)}, f32[1152]{0:T(1024)}, u32[]{:S(2)}) copy-start(f32[1152]{0:T(1024)} %param.24) | copy-start | bytes 13828
  56.9 15.0 %copy-start.8 = (f32[1152]{0:T(1024)S(1)}, f32[1152]{0:T(1024)}, u32[]{:S(2)}) copy-start(f32[1152]{0:T(1024)} %param.25) | copy-start | bytes 13828
  69.3 2.6 %copy-start.2 = (f32[128,1152]{1,0:T(8,128)S(1)}, f32[128,1152]{1,0:T(8,128)}, u32[]{:S(2)}) copy-start(f32[128,1152]{1,0:T(8,128)} %shard_map.146) | copy-start | bytes 1769476
  71.9 13.8 %copy-start.6 = (f32[8,16,128]{2,1,0:T(8,128)S(1)}, f32[8,16,128]{2,1,0:T(8,128)}, u32[]{:S(2)}) copy-start(f32[8,16,128]{2,1,0:T(8,128)} %get-tuple-element.40) | copy-start | bytes 196612
  107.3 2.1 copy-start.3
Sparse Core Ops, SparseCore 0:
  10.1 80.6 all-gather.1

commit v3 on v2

--- a/solution.py
+++ b/solution.py
@@ -330,7 +330,7 @@
 
 def expert_kernel(
     rows_ref, select_ref, shared_ref, gated_ref, tokens_ref, in_ref, down_ref,
-    gate_a_ref, gate_b_ref,
+    gate_a_ref, up_a_ref, gate_b_ref, up_b_ref,
     out_ref,
     ring_ref, chosen_ref, sum_land_ref, sum_stage_ref, slots_ref, weight_ref, hidden_ref, part_ref,
     high_ref, low_ref, side_ref, stage_ref, back_ref, mix_ref, land_ref, step_ref, base_ref,
@@ -350,10 +350,12 @@
         ((0, 0, 1), in_ref.at[1, high_units]),
         ((0, 0, 2), down_ref.at[high_units]),
         ((0, 1, 0), gate_b_ref),
+        ((0, 1, 1), up_b_ref),
         ((1, 0, 0), in_ref.at[0, low_units]),
         ((1, 0, 1), in_ref.at[1, low_units]),
         ((1, 0, 2), down_ref.at[low_units]),
         ((1, 1, 0), gate_a_ref),
+        ((1, 1, 1), up_a_ref),
     ):
         copy = pltpu.make_async_copy(source, weight_ref.at[where], weight_sem.at[len(loads)])
         copy.start()
@@ -407,8 +409,7 @@
 
     shared_step(0)
     swapped = [
-        post.send(source.at[half_units], weight_ref.at[1 - side, 1, kind], across[side])
-        for kind, source in ((1, in_ref.at[1]), (2, down_ref))
+        post.send(down_ref.at[half_units], weight_ref.at[1 - side, 1, 2], across[side])
         for side, half_units in ((0, low_units), (1, high_units))
     ]
     for j in range(CHUNKS):
@@ -618,7 +619,7 @@
     chunk = width // CHUNKS
     kind = rows.dtype
     units = weights[-1].shape[0]
-    copies = CHUNKS * (2 * Z_COPIES + 2 * (GROUP - 1) + 2 * GROUP) + X_COPIES + 4
+    copies = CHUNKS * (2 * Z_COPIES + 2 * (GROUP - 1) + 2 * GROUP) + X_COPIES + 2
     boxes = pltpu.VMEM((CHUNKS, len(Z_STREAMS) * Z_HALF, tokens // 2, chunk), kind)
     blocks = pltpu.VMEM((CHUNKS, GROUP, slots, chunk), kind)
     shared_boxes = pltpu.VMEM((X_COPIES, tokens // 2, width), kind)
@@ -650,7 +651,7 @@
             pltpu.SemaphoreType.DMA((copies,)),
             pltpu.SemaphoreType.DMA((copies,)),
             pltpu.SemaphoreType.DMA((CHUNKS,)),
-            pltpu.SemaphoreType.DMA((8,)),
+            pltpu.SemaphoreType.DMA((10,)),
             pltpu.SemaphoreType.DMA((2 * CHUNKS * GROUP,)),
             pltpu.SemaphoreType.DMA((2 * CHUNKS * GROUP,)),
         ],
@@ -789,6 +790,7 @@
     units = expert_out.shape[1] // 2
     in_rows = expert_in[0].transpose(1, 2, 0)
     gate_halves = in_rows[0, :units], in_rows[0, units:]
+    up_halves = in_rows[1, :units], in_rows[1, units:]
 
     def swap(halves, after):
         first, second, after = lax.optimization_barrier((*halves, after))
@@ -841,6 +843,7 @@
         .reshape(tokens, 4 * width_vit)
     )
     (group_merged,) = ring_gather([("x", merged, 16)], 2)
+    up_a, up_b, group_merged = swap(up_halves, group_merged)
     select, gated = slot_tables(tables_z, tokens, top)
     projected = jnp.dot(
         group_merged.reshape(NX * tokens, -1), project, preferred_element_type=jnp.float32
@@ -863,7 +866,7 @@
         shared_rows,
         gated,
         tokens_moe,
-        (in_rows, expert_out[0], gate_a, gate_b),
+        (in_rows, expert_out[0], gate_a, up_a, gate_b, up_b),
         4,
     )
     return output.reshape(1, row_count // 2, columns // 2, width_moe)

time: 256 us -> 255 us (level)
  starting transfers between devices: 2.18 us -> 5.11 us
  waiting for transfers between devices: 3.33 us -> 0.72 us
    pallas_call x1, Pallas kernels: 134 us -> 120 us  [expert_layer(): pl.pallas_call(expert_kernel, out_shape=jax.ShapeDtypeStruct((tokens, wid...]
    pallas_call x1, Pallas kernels: 12.3 us -> 25.1 us  [gather_tokens(): pl.pallas_call(kernel, out_shape=[jax.ShapeDtypeStruct((tokens, NX * widt...]
    all_gather x1, waiting for transfers between devices: 2.61 us -> 0.01 us  [per_device(): project = lax.all_gather(proj_weight, 'expert', axis=0, tiled=True)]
  transfers between devices with their start and end apart: 3 -> 5, of which waited for: 1 -> 0; matrix products, arithmetic and copies ran while one was open for 15% -> 15% of each run, Pallas kernels for 24% -> 30%
where the time goes in v3:
time: 255 us
  Pallas kernels  195 us (76%)
  matrix products  20.4 us (8%)
  between operations  13.7 us (5%)
  other arithmetic  10.7 us (4%)
  local copies, waits for them, and re-layouts  8.97 us (4%)
  starting transfers between devices  5.11 us (2%)
    pallas_call x1, Pallas kernels, expert_layer(): pl.pallas_call(expert_kernel, out_shape=jax.ShapeDtypeStruct((tokens, wid...  120 us
    pallas_call x2, Pallas kernels, ring_gather(): pl.pallas_call(kernel, out_shape=[jax.ShapeDtypeStruct((sizes[axis],) + b...  38.1 us
    pallas_call x1, Pallas kernels, gather_tokens(): pl.pallas_call(kernel, out_shape=[jax.ShapeDtypeStruct((tokens, NX * widt...  25.1 us
    pallas_call x1, Pallas kernels, ring_reduce(): pl.pallas_call(kernel, out_shape=[jax.ShapeDtypeStruct(block.shape[1:], k...  12 us
  transfers between devices with their start and end apart: 5, of which 0 were waited for; matrix products, arithmetic and copies ran while one was open for 15% of the time, Pallas kernels for 30%

profile of v3, /device:TPU:8, one launch (start us, length us, event | category | flops | bytes accessed | tf_op | source)
XLA Modules:
  0.0 254.6 jit_solution(13801190370801247499)
XLA Ops:
  6.5 0.0 copy-start
  6.5 0.0 all-gather.2.cloned.1.call-start
  6.5 0.7 all-gather.2.cloned.1.call-update
  7.3 1.2 convert_reduce_fusion
  8.5 0.1 div.89
  8.6 1.2 fusion.10
  9.8 0.1 rsqrt.20
  9.9 0.8 reshape.403
  10.7 0.8 reshape.404
  11.5 0.4 scatter.9.refs_1_
  11.9 0.0 copy-start.7
  11.9 1.9 fusion.13.refs_0_
  13.8 0.0 copy-done.7
  13.8 23.7 %shard_map.145 = (bf16[4,128,1152]{2,1,0:T(8,128)(2,1)}, f32[8,16,128]{2,1,0:T(8,128)}) custom-call(bf16[128,1152]{1,0:T(8,128)(2,1)} %fusion.13.refs_0_, f32[16,128]{1,0:T(8,128)} %copy-done.7), custom_call_target="tpu_custom_call" | custom-call | tf_op jit(solution)/shard_map/pallas_call | solution.py:172
  37.5 0.0 copy-start.9
  37.5 3.5 %slice_bitcast_fusion = (bf16[176,2048]{1,0:T(8,128)(2,1)}, bf16[176,2048]{1,0:T(8,128)(2,1)}, bf16[176,2048]{1,0:T(8,128)(2,1)}, bf16[176,2048]{1,0:T(8,128)(2,1)}) fusion(bf16[2,352,2048]{2,1,0:T(8,128)(2,1)} %bitcast.126), kind=kLoop, calls=%fused_computation.14 | loop fusion | bytes 5767168 | tf_op jit(solution)/shard_map/squeeze | solution.py:792
  41.1 0.9 collective-permute-start
  42.0 0.0 copy-done.9
  42.0 0.1 add.156
  42.1 0.4 multiply_cosine_fusion.1
  42.5 3.3 %convolution_add_fusion = f32[512,3,4,72]{0,3,2,1:T(8,128)S(1)} fusion(bf16[512,1152,1,1]{1,0,3,2:T(8,128)(2,1)} %bitcast.137, bf16[3,4,72,1152]{3,2,1,0:T(8,128)(2,1)} %bitcast.136, f32[3,4,72]{2,1,0:T(4,128)S(1)} %add.156), kind=kOutput, calls=%fused_computation.11 | convolution fusion | flops 1019658240 | bytes 4943232 | tf_op jit(solution)/shard_map/dot_general | solution.py:818
  45.8 0.1 slice_bitcast_fusion.5
  45.9 0.1 subtract_convert_fusion.1
  46.0 1.0 subtract_convert_fusion.3
  47.0 4.5 %fusion.57 = (f32[4,512]{1,0:T(4,128)S(1)}, f32[4,512,512]{1,2,0:T(8,128)}) fusion(bf16[512,4,18]{0,2,1:T(8,128)(2,1)S(1)} %get-tuple-element.67, bf16[512,4,18]{0,2,1:T(8,128)(2,1)S(1)} %get-tuple-element.68, bf16[512,4,18]{0,2,1:T(8,128)(2,1)S(1)} %get-tuple-element.62, bf16[512,4,18]{0,2,1:T(8,128)(2,1)S(1)} %get-tuple-element.61, ...), kind=kOutput, calls=%fused_computation.119 | convolution fusion | flops 156500480 | bytes 4792320 | tf_op jit(solution)/shard_map/sub | solution.py:58
  51.6 2.9 %fusion.8 = bf16[4,72,512]{2,1,0:T(8,128)(2,1)S(1)} fusion(f32[4,512,512]{1,2,0:T(8,128)} %get-tuple-element.78, f32[4,512]{1,0:T(4,128)S(1)} %get-tuple-element.77, f32[512,3,4,72]{0,3,2,1:T(8,128)} %copy-done.4), kind=kOutput, calls=%fused_computation.12 | convolution fusion | flops 153239552 | bytes 4792320 | tf_op jit(solution)/shard_map/hqk,khd->qhd/dot_general | solution.py:59
  54.5 0.0 copy-done.10
  54.5 0.0 copy-start.1
  54.5 0.0 copy-start.5
  54.5 1.9 convolution_convert_fusion
  56.4 12.0 %shard_map.146 = f32[128,1152]{1,0:T(8,128)} custom-call(bf16[4,128,1152]{2,1,0:T(8,128)(2,1)} %bitcast.131), custom_call_target="tpu_custom_call" | custom-call | tf_op jit(solution)/shard_map/pallas_call | solution.py:268
  68.4 0.0 copy-done.1
  68.5 0.0 copy-done.5
  68.5 0.0 copy-start.2
  68.5 1.3 fusion.28
  69.8 1.3 multiply_reduce_fusion.1
  71.1 0.2 multiply_convert_fusion
  71.2 0.1 reshape.409
  71.4 0.2 copy.35
  71.6 0.9 reshape.410.refs_0_
  72.5 14.3 %shard_map.147 = bf16[4,32,4608]{2,1,0:T(8,128)(2,1)} custom-call(bf16[32,4608]{1,0:T(8,128)(2,1)} %reshape.410.refs_0_), custom_call_target="tpu_custom_call" | custom-call | tf_op jit(solution)/shard_map/pallas_call | solution.py:172
  86.8 1.0 collective-permute-start.1
  87.8 2.4 collective-permute-start.2
  90.2 0.9 collective-permute-start.3
  91.0 0.1 eq.87
  91.2 0.1 eq.77
  91.2 0.1 broadcast_in_dim.20
  91.4 0.1 compare_reduce_fusion
  91.4 0.2 fusion.24
  91.7 0.1 broadcast_compare_fusion
  91.7 0.8 fusion.20.select_ref
  92.6 0.1 fusion.33
  92.7 0.9 bitcast_select_fusion.gated_ref
  93.6 4.1 %convolution_convert_fusion.2.refs_0_ = bf16[128,512]{1,0:T(8,128)(2,1)} fusion(bf16[128,4608]{1,0:T(8,128)(2,1)} %bitcast.128, bf16[4608,512]{1,0:T(8,128)(2,1)} %all-gather.2.cloned.1.call-done), kind=kOutput, calls=%fused_computation.13 | convolution fusion | flops 604045312 | bytes 6029312 | tf_op jit(solution)/shard_map/dot_general | solution.py:848
  97.7 25.1 %shard_map.148 = (bf16[32,2048]{1,0:T(8,128)(2,1)}, bf16[32,2048]{1,0:T(8,128)(2,1)}, bf16[128,2048]{1,0:T(8,128)(2,1)}) custom-call(bf16[128,512]{1,0:T(8,128)(2,1)} %convolution_convert_fusion.2.refs_0_, f32[1,2048]{1,0:T(1,128)} %bitcast.135), custom_call_target="tpu_custom_call" | custom-call | tf_op jit(solution)/shard_map/pallas_call | solution.py:721
  122.8 0.0 copy-start.3
  122.9 2.1 fusion.4
  124.9 1.4 convolution_convert_fusion.1
  126.3 0.0 collective-permute-done.gate_a_ref
  126.3 0.0 collective-permute-done.1.up_a_ref
  126.3 0.0 collective-permute-done.2.gate_b_ref
  126.3 0.0 collective-permute-done.3.up_b_ref
  126.3 119.8 %shard_map.149 = bf16[32,2048]{1,0:T(8,128)(2,1)} custom-call(bf16[32,2048]{1,0:T(8,128)(2,1)} %get-tuple-element.43.rows_ref, bf16[384,256]{1,0:T(8,128)(2,1)} %fusion.20.select_ref, bf16[4,32,2048]{2,1,0:T(8,128)(2,1)} %bitcast.129, f32[384,256]{1,0:T(8,128)} %bitcast_select_fusion.gated_ref, bf16[32,2048]{1,0:T(8,128)(2,1)} %get-tuple-element.46.tokens_ref, ...), custom_call_target="tpu_custom_call" | custom-call | tf_op jit(solution)/shard_map/pallas_call | solution.py:627
  246.1 1.6 copy.38
  (28 shorter events, 0.1 us)
Async XLA Ops:
  6.5 116.3 %copy-start = (bf16[2048,2,352]{0,2,1:T(8,128)(2,1)S(1)}, bf16[2048,2,352]{0,2,1:T(8,128)(2,1)}, u32[]{:S(2)}) copy-start(bf16[2048,2,352]{0,2,1:T(8,128)(2,1)} %param.30) | copy-start | bytes 8650756
  6.5 87.0 %all-gather.2.cloned.1.call-start = ((), (), s32[]{:S(2)}) async-start(), calls=%async_computation | async-start | bytes 4792320 | tf_op jit(solution)/shard_map/all_gather | solution.py:801
  11.9 1.9 copy-start.7
  37.5 4.4 %copy-start.9 = (f32[3,288]{1,0:T(4,128)S(1)}, f32[3,288]{1,0:T(4,128)}, u32[]{:S(2)}) copy-start(f32[3,288]{1,0:T(4,128)} %param.22) | copy-start | bytes 10372
  41.1 85.2 %collective-permute-start = (bf16[176,2048]{1,0:T(8,128)(2,1)}, bf16[176,2048]{1,0:T(8,128)(2,1)}, u32[]{:S(2)}, u32[]{:S(2)}) collective-permute-start(bf16[176,2048]{1,0:T(8,128)(2,1)} %get-tuple-element.47), channel_id=1, source_target_pairs={{0,64},{64,0},{128,192},{192,128},{1,65},{65,1},{129,193},{193,129... | collective-permute-start | bytes 2162696 | tf_op jit(solution)/shard_map/ppermute | solution.py:797
  45.8 1.3 copy-start.4
  51.6 2.9 %copy-start.10 = (bf16[288,1152]{1,0:T(8,128)(2,1)S(1)}, bf16[288,1152]{1,0:T(8,128)(2,1)}, u32[]{:S(2)}) copy-start(bf16[288,1152]{1,0:T(8,128)(2,1)} %param.23) | copy-start | bytes 1990660
  54.5 13.9 %copy-start.1 = (bf16[1,4,32,1152]{3,2,1,0:T(8,128)(2,1)S(1)}, bf16[1,4,32,1152]{3,2,1,0:T(8,128)(2,1)}, u32[]{:S(2)}) copy-start(bf16[1,4,32,1152]{3,2,1,0:T(8,128)(2,1)} %param.19) | copy-start | bytes 884740
  54.5 13.9 %copy-start.5 = (f32[1152]{0:T(1024)S(1)}, f32[1152]{0:T(1024)}, u32[]{:S(2)}) copy-start(f32[1152]{0:T(1024)} %param.24) | copy-start | bytes 13828
  56.4 14.6 %copy-start.8 = (f32[1152]{0:T(1024)S(1)}, f32[1152]{0:T(1024)}, u32[]{:S(2)}) copy-start(f32[1152]{0:T(1024)} %param.25) | copy-start | bytes 13828
  68.5 2.6 %copy-start.2 = (f32[128,1152]{1,0:T(8,128)S(1)}, f32[128,1152]{1,0:T(8,128)}, u32[]{:S(2)}) copy-start(f32[128,1152]{1,0:T(8,128)} %shard_map.146) | copy-start | bytes 1769476
  71.1 20.1 %copy-start.6 = (f32[8,16,128]{2,1,0:T(8,128)S(1)}, f32[8,16,128]{2,1,0:T(8,128)}, u32[]{:S(2)}) copy-start(f32[8,16,128]{2,1,0:T(8,128)} %get-tuple-element.44) | copy-start | bytes 196612
  86.8 39.5 %collective-permute-start.1 = (bf16[176,2048]{1,0:T(8,128)(2,1)}, bf16[176,2048]{1,0:T(8,128)(2,1)}, u32[]{:S(2)}, u32[]{:S(2)}) collective-permute-start(bf16[176,2048]{1,0:T(8,128)(2,1)} %get-tuple-element.48), channel_id=1, source_target_pairs={{0,64},{64,0},{128,192},{192,128},{1,65},{65,1},{129,193},{193,129... | collective-permute-start | bytes 2162696 | tf_op jit(solution)/shard_map/ppermute | solution.py:797
  87.8 38.5 %collective-permute-start.2 = (bf16[176,2048]{1,0:T(8,128)(2,1)}, bf16[176,2048]{1,0:T(8,128)(2,1)}, u32[]{:S(2)}, u32[]{:S(2)}) collective-permute-start(bf16[176,2048]{1,0:T(8,128)(2,1)} %get-tuple-element.49), channel_id=1, source_target_pairs={{0,192},{64,128},{128,64},{192,0},{1,193},{65,129},{129,65},{193,1... | collective-permute-start | bytes 2162696 | tf_op jit(solution)/shard_map/ppermute | solution.py:798
  90.2 36.2 %collective-permute-start.3 = (bf16[176,2048]{1,0:T(8,128)(2,1)}, bf16[176,2048]{1,0:T(8,128)(2,1)}, u32[]{:S(2)}, u32[]{:S(2)}) collective-permute-start(bf16[176,2048]{1,0:T(8,128)(2,1)} %get-tuple-element.50), channel_id=1, source_target_pairs={{0,192},{64,128},{128,64},{192,0},{1,193},{65,129},{129,65},{193,1... | collective-permute-start | bytes 2162696 | tf_op jit(solution)/shard_map/ppermute | solution.py:798
  122.8 2.1 copy-start.3
Sparse Core Ops, SparseCore 0:
  10.1 80.9 all-gather.1

commit v4 on v3

--- a/solution.py
+++ b/solution.py
@@ -423,7 +423,8 @@
 
     def hand_on(j, k, source):
         for side in (0, 1):
-            handed.append(post.send(source, slots_ref.at[2 * side, k, :, cols[j]], across[side]))
+            copy = post.send(source, slots_ref.at[2 * side, k, :, cols[j]], across[side])
+            handed.append((k // PER_JOB, copy))
 
     def choose(j):
         for sign, half, _ in Z_STREAMS:
@@ -511,8 +512,6 @@
         return carry
 
     lax.fori_loop(0, 4, own_job, 0)
-    for copy in handed:
-        copy.wait_recv()
 
     def side_job(i, carry):
         which, job = i % 2, i // 2
@@ -522,7 +521,11 @@
                 side_copy(which, j, job * PER_JOB + k).start()
         return carry
 
-    lax.fori_loop(0, 4, side_job, 0)
+    for job in (0, 1):
+        for this, copy in handed:
+            if this == job:
+                copy.wait_recv()
+        lax.fori_loop(2 * job, 2 * job + 2, side_job, 0)
 
     for half in (0, 1):
         total = shared_ref[tile, part[half]].astype(jnp.float32)

time: 255 us -> 250 us (0.980)
  Pallas kernels: 195 us -> 190 us
    pallas_call x1, Pallas kernels: 120 us -> 115 us  [expert_layer(): pl.pallas_call(expert_kernel, out_shape=jax.ShapeDtypeStruct((tokens, wid...]
where the time goes in v4:
time: 250 us
  Pallas kernels  190 us (76%)
  matrix products  20.4 us (8%)
  between operations  13.7 us (5%)
  other arithmetic  10.7 us (4%)
  local copies, waits for them, and re-layouts  8.97 us (4%)
  starting transfers between devices  5.11 us (2%)
    pallas_call x1, Pallas kernels, expert_layer(): pl.pallas_call(expert_kernel, out_shape=jax.ShapeDtypeStruct((tokens, wid...  115 us
    pallas_call x2, Pallas kernels, ring_gather(): pl.pallas_call(kernel, out_shape=[jax.ShapeDtypeStruct((sizes[axis],) + b...  38.1 us
    pallas_call x1, Pallas kernels, gather_tokens(): pl.pallas_call(kernel, out_shape=[jax.ShapeDtypeStruct((tokens, NX * widt...  25.1 us
    pallas_call x1, Pallas kernels, ring_reduce(): pl.pallas_call(kernel, out_shape=[jax.ShapeDtypeStruct(block.shape[1:], k...  12 us
  transfers between devices with their start and end apart: 5, of which 0 were waited for; matrix products, arithmetic and copies ran while one was open for 15% of the time, Pallas kernels for 30%

profile of v4, /device:TPU:8, one launch (start us, length us, event | category | flops | bytes accessed | tf_op | source)
XLA Modules:
  0.0 249.6 jit_solution(14586454803687794333)
XLA Ops:
  6.5 0.0 copy-start
  6.5 0.0 all-gather.2.cloned.1.call-start
  6.5 0.7 all-gather.2.cloned.1.call-update
  7.3 1.2 convert_reduce_fusion
  8.5 0.1 div.89
  8.6 1.2 fusion.10
  9.8 0.1 rsqrt.20
  9.9 0.8 reshape.403
  10.7 0.8 reshape.404
  11.5 0.4 scatter.9.refs_1_
  11.9 0.0 copy-start.7
  11.9 1.9 fusion.13.refs_0_
  13.8 0.0 copy-done.7
  13.8 23.7 %shard_map.145 = (bf16[4,128,1152]{2,1,0:T(8,128)(2,1)}, f32[8,16,128]{2,1,0:T(8,128)}) custom-call(bf16[128,1152]{1,0:T(8,128)(2,1)} %fusion.13.refs_0_, f32[16,128]{1,0:T(8,128)} %copy-done.7), custom_call_target="tpu_custom_call" | custom-call | tf_op jit(solution)/shard_map/pallas_call | solution.py:172
  37.5 0.0 copy-start.9
  37.5 3.5 %slice_bitcast_fusion = (bf16[176,2048]{1,0:T(8,128)(2,1)}, bf16[176,2048]{1,0:T(8,128)(2,1)}, bf16[176,2048]{1,0:T(8,128)(2,1)}, bf16[176,2048]{1,0:T(8,128)(2,1)}) fusion(bf16[2,352,2048]{2,1,0:T(8,128)(2,1)} %bitcast.126), kind=kLoop, calls=%fused_computation.14 | loop fusion | bytes 5767168 | tf_op jit(solution)/shard_map/squeeze | solution.py:795
  41.1 0.9 collective-permute-start
  42.0 0.0 copy-done.9
  42.0 0.1 add.156
  42.1 0.4 multiply_cosine_fusion.1
  42.5 3.3 %convolution_add_fusion = f32[512,3,4,72]{0,3,2,1:T(8,128)S(1)} fusion(bf16[512,1152,1,1]{1,0,3,2:T(8,128)(2,1)} %bitcast.137, bf16[3,4,72,1152]{3,2,1,0:T(8,128)(2,1)} %bitcast.136, f32[3,4,72]{2,1,0:T(4,128)S(1)} %add.156), kind=kOutput, calls=%fused_computation.11 | convolution fusion | flops 1019658240 | bytes 4943232 | tf_op jit(solution)/shard_map/dot_general | solution.py:821
  45.8 0.1 slice_bitcast_fusion.5
  45.9 0.1 subtract_convert_fusion.1
  46.0 1.0 subtract_convert_fusion.3
  47.0 4.5 %fusion.57 = (f32[4,512]{1,0:T(4,128)S(1)}, f32[4,512,512]{1,2,0:T(8,128)}) fusion(bf16[512,4,18]{0,2,1:T(8,128)(2,1)S(1)} %get-tuple-element.67, bf16[512,4,18]{0,2,1:T(8,128)(2,1)S(1)} %get-tuple-element.68, bf16[512,4,18]{0,2,1:T(8,128)(2,1)S(1)} %get-tuple-element.62, bf16[512,4,18]{0,2,1:T(8,128)(2,1)S(1)} %get-tuple-element.61, ...), kind=kOutput, calls=%fused_computation.119 | convolution fusion | flops 156500480 | bytes 4792320 | tf_op jit(solution)/shard_map/sub | solution.py:58
  51.6 2.9 %fusion.8 = bf16[4,72,512]{2,1,0:T(8,128)(2,1)S(1)} fusion(f32[4,512,512]{1,2,0:T(8,128)} %get-tuple-element.78, f32[4,512]{1,0:T(4,128)S(1)} %get-tuple-element.77, f32[512,3,4,72]{0,3,2,1:T(8,128)} %copy-done.4), kind=kOutput, calls=%fused_computation.12 | convolution fusion | flops 153239552 | bytes 4792320 | tf_op jit(solution)/shard_map/hqk,khd->qhd/dot_general | solution.py:59
  54.5 0.0 copy-done.10
  54.5 0.0 copy-start.1
  54.5 0.0 copy-start.5
  54.5 1.9 convolution_convert_fusion
  56.4 12.0 %shard_map.146 = f32[128,1152]{1,0:T(8,128)} custom-call(bf16[4,128,1152]{2,1,0:T(8,128)(2,1)} %bitcast.131), custom_call_target="tpu_custom_call" | custom-call | tf_op jit(solution)/shard_map/pallas_call | solution.py:268
  68.4 0.0 copy-done.1
  68.5 0.0 copy-done.5
  68.5 0.0 copy-start.2
  68.5 1.3 fusion.28
  69.8 1.3 multiply_reduce_fusion.1
  71.1 0.2 multiply_convert_fusion
  71.2 0.1 reshape.409
  71.4 0.2 copy.35
  71.6 0.9 reshape.410.refs_0_
  72.5 14.3 %shard_map.147 = bf16[4,32,4608]{2,1,0:T(8,128)(2,1)} custom-call(bf16[32,4608]{1,0:T(8,128)(2,1)} %reshape.410.refs_0_), custom_call_target="tpu_custom_call" | custom-call | tf_op jit(solution)/shard_map/pallas_call | solution.py:172
  86.8 1.0 collective-permute-start.1
  87.8 2.4 collective-permute-start.2
  90.2 0.9 collective-permute-start.3
  91.0 0.1 eq.87
  91.2 0.1 eq.77
  91.2 0.1 broadcast_in_dim.20
  91.4 0.1 compare_reduce_fusion
  91.4 0.2 fusion.24
  91.7 0.1 broadcast_compare_fusion
  91.7 0.8 fusion.20.select_ref
  92.6 0.1 fusion.33
  92.7 0.9 bitcast_select_fusion.gated_ref
  93.6 4.1 %convolution_convert_fusion.2.refs_0_ = bf16[128,512]{1,0:T(8,128)(2,1)} fusion(bf16[128,4608]{1,0:T(8,128)(2,1)} %bitcast.128, bf16[4608,512]{1,0:T(8,128)(2,1)} %all-gather.2.cloned.1.call-done), kind=kOutput, calls=%fused_computation.13 | convolution fusion | flops 604045312 | bytes 6029312 | tf_op jit(solution)/shard_map/dot_general | solution.py:851
  97.7 25.1 %shard_map.148 = (bf16[32,2048]{1,0:T(8,128)(2,1)}, bf16[32,2048]{1,0:T(8,128)(2,1)}, bf16[128,2048]{1,0:T(8,128)(2,1)}) custom-call(bf16[128,512]{1,0:T(8,128)(2,1)} %convolution_convert_fusion.2.refs_0_, f32[1,2048]{1,0:T(1,128)} %bitcast.135), custom_call_target="tpu_custom_call" | custom-call | tf_op jit(solution)/shard_map/pallas_call | solution.py:724
  122.8 0.0 copy-start.3
  122.9 2.1 fusion.4
  124.9 1.4 convolution_convert_fusion.1
  126.3 0.0 collective-permute-done.gate_a_ref
  126.3 0.0 collective-permute-done.1.up_a_ref
  126.3 0.0 collective-permute-done.2.gate_b_ref
  126.3 0.0 collective-permute-done.3.up_b_ref
  126.3 114.8 %shard_map.149 = bf16[32,2048]{1,0:T(8,128)(2,1)} custom-call(bf16[32,2048]{1,0:T(8,128)(2,1)} %get-tuple-element.43.rows_ref, bf16[384,256]{1,0:T(8,128)(2,1)} %fusion.20.select_ref, bf16[4,32,2048]{2,1,0:T(8,128)(2,1)} %bitcast.129, f32[384,256]{1,0:T(8,128)} %bitcast_select_fusion.gated_ref, bf16[32,2048]{1,0:T(8,128)(2,1)} %get-tuple-element.46.tokens_ref, ...), custom_call_target="tpu_custom_call" | custom-call | tf_op jit(solution)/shard_map/pallas_call | solution.py:630
  241.2 1.6 copy.38
  (28 shorter events, 0.1 us)
Async XLA Ops:
  6.5 116.3 %copy-start = (bf16[2048,2,352]{0,2,1:T(8,128)(2,1)S(1)}, bf16[2048,2,352]{0,2,1:T(8,128)(2,1)}, u32[]{:S(2)}) copy-start(bf16[2048,2,352]{0,2,1:T(8,128)(2,1)} %param.30) | copy-start | bytes 8650756
  6.5 87.0 %all-gather.2.cloned.1.call-start = ((), (), s32[]{:S(2)}) async-start(), calls=%async_computation | async-start | bytes 4792320 | tf_op jit(solution)/shard_map/all_gather | solution.py:804
  11.9 1.9 copy-start.7
  37.5 4.4 %copy-start.9 = (f32[3,288]{1,0:T(4,128)S(1)}, f32[3,288]{1,0:T(4,128)}, u32[]{:S(2)}) copy-start(f32[3,288]{1,0:T(4,128)} %param.22) | copy-start | bytes 10372
  41.1 85.2 %collective-permute-start = (bf16[176,2048]{1,0:T(8,128)(2,1)}, bf16[176,2048]{1,0:T(8,128)(2,1)}, u32[]{:S(2)}, u32[]{:S(2)}) collective-permute-start(bf16[176,2048]{1,0:T(8,128)(2,1)} %get-tuple-element.47), channel_id=1, source_target_pairs={{0,64},{64,0},{128,192},{192,128},{1,65},{65,1},{129,193},{193,129... | collective-permute-start | bytes 2162696 | tf_op jit(solution)/shard_map/ppermute | solution.py:800
  45.8 1.3 copy-start.4
  51.6 2.9 %copy-start.10 = (bf16[288,1152]{1,0:T(8,128)(2,1)S(1)}, bf16[288,1152]{1,0:T(8,128)(2,1)}, u32[]{:S(2)}) copy-start(bf16[288,1152]{1,0:T(8,128)(2,1)} %param.23) | copy-start | bytes 1990660
  54.5 13.9 %copy-start.1 = (bf16[1,4,32,1152]{3,2,1,0:T(8,128)(2,1)S(1)}, bf16[1,4,32,1152]{3,2,1,0:T(8,128)(2,1)}, u32[]{:S(2)}) copy-start(bf16[1,4,32,1152]{3,2,1,0:T(8,128)(2,1)} %param.19) | copy-start | bytes 884740
  54.5 13.9 %copy-start.5 = (f32[1152]{0:T(1024)S(1)}, f32[1152]{0:T(1024)}, u32[]{:S(2)}) copy-start(f32[1152]{0:T(1024)} %param.24) | copy-start | bytes 13828
  56.4 14.6 %copy-start.8 = (f32[1152]{0:T(1024)S(1)}, f32[1152]{0:T(1024)}, u32[]{:S(2)}) copy-start(f32[1152]{0:T(1024)} %param.25) | copy-start | bytes 13828
  68.5 2.6 %copy-start.2 = (f32[128,1152]{1,0:T(8,128)S(1)}, f32[128,1152]{1,0:T(8,128)}, u32[]{:S(2)}) copy-start(f32[128,1152]{1,0:T(8,128)} %shard_map.146) | copy-start | bytes 1769476
  71.1 20.1 %copy-start.6 = (f32[8,16,128]{2,1,0:T(8,128)S(1)}, f32[8,16,128]{2,1,0:T(8,128)}, u32[]{:S(2)}) copy-start(f32[8,16,128]{2,1,0:T(8,128)} %get-tuple-element.44) | copy-start | bytes 196612
  86.8 39.5 %collective-permute-start.1 = (bf16[176,2048]{1,0:T(8,128)(2,1)}, bf16[176,2048]{1,0:T(8,128)(2,1)}, u32[]{:S(2)}, u32[]{:S(2)}) collective-permute-start(bf16[176,2048]{1,0:T(8,128)(2,1)} %get-tuple-element.48), channel_id=1, source_target_pairs={{0,64},{64,0},{128,192},{192,128},{1,65},{65,1},{129,193},{193,129... | collective-permute-start | bytes 2162696 | tf_op jit(solution)/shard_map/ppermute | solution.py:800
  87.8 38.5 %collective-permute-start.2 = (bf16[176,2048]{1,0:T(8,128)(2,1)}, bf16[176,2048]{1,0:T(8,128)(2,1)}, u32[]{:S(2)}, u32[]{:S(2)}) collective-permute-start(bf16[176,2048]{1,0:T(8,128)(2,1)} %get-tuple-element.49), channel_id=1, source_target_pairs={{0,192},{64,128},{128,64},{192,0},{1,193},{65,129},{129,65},{193,1... | collective-permute-start | bytes 2162696 | tf_op jit(solution)/shard_map/ppermute | solution.py:801
  90.2 36.2 %collective-permute-start.3 = (bf16[176,2048]{1,0:T(8,128)(2,1)}, bf16[176,2048]{1,0:T(8,128)(2,1)}, u32[]{:S(2)}, u32[]{:S(2)}) collective-permute-start(bf16[176,2048]{1,0:T(8,128)(2,1)} %get-tuple-element.50), channel_id=1, source_target_pairs={{0,192},{64,128},{128,64},{192,0},{1,193},{65,129},{129,65},{193,1... | collective-permute-start | bytes 2162696 | tf_op jit(solution)/shard_map/ppermute | solution.py:801
  122.8 2.1 copy-start.3
Sparse Core Ops, SparseCore 0:
  10.1 80.9 all-gather.1
